TPU v7x, 512 devices: a whole 4x4x16 slice. The times are simulated.
512 devices in a mesh: dp: 8 (over y, z_hi), tensor: 64 (over x, z_lo, core).
Axes of the slice: x: 4, y: 4, z: 16 (z_hi: 2, z_lo: 8; z = z_hi * 8 + z_lo), core: 2. Of those that a mesh axis runs over, the one named last changes fastest.
Arguments:
- tokens: bfloat16 [8192, 8192], P('dp', 'tensor'), may hold values from -6 to 6
- first_up: bfloat16 [64, 128, 128], P('tensor'), may hold values from -0.5 to 0.5
- second_up: bfloat16 [128, 64, 256], P('tensor'), may hold values from -0.75 to 0.75
- first_down: bfloat16 [128, 256, 64], P('tensor'), may hold values from -0.375 to 0.375
- second_down: bfloat16 [64, 128, 128], P('tensor'), may hold values from -0.5 to 0.5
- out_grad: bfloat16 [8192, 8192], P('dp', 'tensor'), may hold values from -6 to 6
Outputs:
- output: bfloat16 [8192, 8192], P('dp', 'tensor')
- tokens_grad: bfloat16 [8192, 8192], P('dp', 'tensor')
- first_up_grad: float32 [64, 128, 128], P('tensor')
- second_up_grad: float32 [128, 64, 256], P('tensor')
- first_down_grad: float32 [128, 256, 64], P('tensor')
- second_down_grad: float32 [64, 128, 128], P('tensor')
All inputs are finite; a program needn't handle non-finite values.
Results may differ from a plain program's by a relative error of at most 0.0095.
Values may be sent and summed in bfloat16 or wider, within the bound.
A program may use at most 64 MiB of HBM per device.

v0:
```python
import math

import jax
import jax.numpy as jnp
from jax import lax
from jax.sharding import PartitionSpec as P


def cdf_part(value):
    return 0.5 * (1.0 + jax.scipy.special.erf(value / math.sqrt(2.0)))


def gelu_deriv(value):
    return cdf_part(value) + value * jnp.exp(-0.5 * value * value) / math.sqrt(2.0 * math.pi)


def middle_work(upper_cols, second_up, first_down):
    f32 = jnp.float32
    bf16 = jnp.bfloat16
    pre = jnp.einsum("jbt,jbo->jot", upper_cols, second_up, preferred_element_type=f32).astype(bf16)
    prefl = pre.astype(f32)
    act = (prefl * cdf_part(prefl)).astype(bf16)
    zeta = jnp.einsum("jot,job->jbt", act, first_down, preferred_element_type=f32).astype(bf16)
    return (pre, act, zeta)


def column_backward(dzeta_cols, act, pre, upper_cols, second_up, first_down):
    f32 = jnp.float32
    bf16 = jnp.bfloat16
    grad_d1 = jnp.einsum("jot,jbt->job", act, dzeta_cols, preferred_element_type=f32)
    dact = jnp.einsum("jbt,job->jot", dzeta_cols, first_down, preferred_element_type=f32)
    dpre = (dact * gelu_deriv(pre.astype(f32))).astype(bf16)
    grad_u2 = jnp.einsum("jbt,jot->jbo", upper_cols, dpre, preferred_element_type=f32)
    dupper = jnp.einsum("jot,jbo->jbt", dpre, second_up, preferred_element_type=f32).astype(bf16)
    return (grad_d1, grad_u2, dupper)


def shards(tokens, first_up, second_up, first_down, second_down, out_grad):
    f32 = jnp.float32
    bf16 = jnp.bfloat16
    tok_rows = tokens.shape[0]
    local_blocks = first_up.shape[0]
    blk_width = first_up.shape[1]
    xblk = tokens.reshape(tok_rows, local_blocks, blk_width)
    eblk = out_grad.reshape(tok_rows, local_blocks, blk_width)
    upper = jnp.einsum("tbi,bij->jbt", xblk, first_up, preferred_element_type=f32).astype(bf16)
    upper_cols = lax.all_to_all(upper, "tensor", split_axis=0, concat_axis=1, tiled=True)
    pre, act, zeta = middle_work(upper_cols, second_up, first_down)
    zeta_rows = lax.all_to_all(zeta, "tensor", split_axis=1, concat_axis=0, tiled=True)
    grad_d2 = jnp.einsum("jbt,tbk->bjk", zeta_rows, eblk, preferred_element_type=f32)
    dzeta = jnp.einsum("tbk,bjk->jbt", eblk, second_down, preferred_element_type=f32).astype(bf16)
    dzeta_cols = lax.all_to_all(dzeta, "tensor", split_axis=0, concat_axis=1, tiled=True)
    grad_d1, grad_u2, dupper = column_backward(
        dzeta_cols, act, pre, upper_cols, second_up, first_down
    )
    dupper_rows = lax.all_to_all(dupper, "tensor", split_axis=1, concat_axis=0, tiled=True)
    output = jnp.einsum("jbt,bjk->tbk", zeta_rows, second_down, preferred_element_type=f32).astype(
        bf16
    )
    output = output.reshape(tok_rows, local_blocks * blk_width)
    grad_u1 = jnp.einsum("tbi,jbt->bij", xblk, dupper_rows, preferred_element_type=f32)
    grad_u1, grad_u2, grad_d1, grad_d2 = lax.psum((grad_u1, grad_u2, grad_d1, grad_d2), "dp")
    tokens_grad = jnp.einsum(
        "jbt,bij->tbi", dupper_rows, first_up, preferred_element_type=f32
    ).astype(bf16)
    tokens_grad = tokens_grad.reshape(tok_rows, local_blocks * blk_width)
    return (output, tokens_grad, grad_u1, grad_u2, grad_d1, grad_d2)


def solution(mesh):
    placed = (
        P("dp", "tensor"),
        P("tensor", None, None),
        P("tensor", None, None),
        P("tensor", None, None),
        P("tensor", None, None),
        P("dp", "tensor"),
    )
    return jax.shard_map(
        shards,
        mesh=mesh,
        in_specs=placed,
        out_specs=(
            P("dp", "tensor"),
            P("dp", "tensor"),
            P("tensor", None, None),
            P("tensor", None, None),
            P("tensor", None, None),
            P("tensor", None, None),
        ),
        check_vma=False,
    )
```

profile of v0, /device:TPU:102, one launch (start us, length us, event | category | flops | bytes accessed | tf_op | source)
XLA Modules:
  0.0 323.2 jit_solution(2137689660007310916)
XLA Ops:
  7.2 0.0 copy-start
  7.2 0.0 copy-start.3
  7.2 0.9 copy-done
  8.1 1.0 fusion.12
  9.1 0.5 broadcast.19
  9.6 0.8 reduce.2
  10.4 0.8 reshape.62
  11.2 14.9 %all-to-all-start = ((bf16[64,2,1024]{2,1,0:T(2,128)(2,1)}), bf16[64,2,1024]{2,1,0:T(2,128)(2,1)S(1)}, u32[]{:S(2)}, u32[]{:S(2)}) async-start(bf16[64,2,1024]{2,1,0:T(2,128)(2,1)} %reshape.62), calls=%async_computation | async-start | bytes 524288 | tf_op jit(solution)/shard_map/all_to_all | solution.py:47
  26.2 0.2 fusion.13
  26.4 0.8 reduce.3
  27.2 0.8 reshape.64
  28.0 13.2 %all-to-all-done = bf16[64,2,1024]{2,1,0:T(2,128)(2,1)S(1)} async-done(((bf16[64,2,1024]{2,1,0:T(2,128)(2,1)}), bf16[64,2,1024]{2,1,0:T(2,128)(2,1)S(1)}, u32[]{:S(2)}, u32[]{:S(2)}) %all-to-all-start) | async-done | bytes 262176 | tf_op jit(solution)/shard_map/all_to_all | solution.py:47
  41.2 11.1 %all-to-all-start.2 = ((bf16[64,2,1024]{2,1,0:T(2,128)(2,1)}), bf16[64,2,1024]{2,1,0:T(2,128)(2,1)S(1)}, u32[]{:S(2)}, u32[]{:S(2)}) async-start(bf16[64,2,1024]{2,1,0:T(2,128)(2,1)} %reshape.64), calls=%async_computation.2 | async-start | bytes 524288 | tf_op jit(solution)/shard_map/all_to_all | solution.py:52
  52.3 0.0 copy-start.4
  52.3 0.2 reshape.63
  52.6 1.5 reduce
  54.1 0.8 all_to_all.49
  54.9 12.5 %all-to-all-done.2 = bf16[64,2,1024]{2,1,0:T(2,128)(2,1)S(1)} async-done(((bf16[64,2,1024]{2,1,0:T(2,128)(2,1)}), bf16[64,2,1024]{2,1,0:T(2,128)(2,1)S(1)}, u32[]{:S(2)}, u32[]{:S(2)}) %all-to-all-start.2) | async-done | bytes 262176 | tf_op jit(solution)/shard_map/all_to_all | solution.py:52
  67.4 0.2 reshape.65
  67.6 1.5 reduce.1
  69.1 0.8 all_to_all.56
  69.9 0.0 copy-done.4
  70.0 1.5 fusion.8
  71.5 0.8 fusion.5
  72.4 1.0 copy-done.1
  73.3 0.4 fusion.11
  73.8 1.0 copy.44
  74.7 11.3 %all-to-all-start.3 = ((bf16[2,64,1024]{2,0,1:T(2,128)(2,1)}), bf16[2,64,1024]{2,0,1:T(2,128)(2,1)}, u32[]{:S(2)}, u32[]{:S(2)}) async-start(bf16[2,64,1024]{2,0,1:T(2,128)(2,1)} %copy.44), calls=%async_computation.3 | async-start | bytes 524288 | tf_op jit(solution)/shard_map/all_to_all | solution.py:56
  86.1 1.3 fusion.10
  87.3 1.0 copy.40
  88.3 12.7 %all-to-all-done.3 = bf16[2,64,1024]{2,0,1:T(2,128)(2,1)} async-done(((bf16[2,64,1024]{2,0,1:T(2,128)(2,1)}), bf16[2,64,1024]{2,0,1:T(2,128)(2,1)}, u32[]{:S(2)}, u32[]{:S(2)}) %all-to-all-start.3) | async-done | bytes 262176 | tf_op jit(solution)/shard_map/all_to_all | solution.py:56
  101.0 11.3 %all-to-all-start.1 = ((bf16[2,64,1024]{2,0,1:T(2,128)(2,1)}), bf16[2,64,1024]{2,0,1:T(2,128)(2,1)}, u32[]{:S(2)}, u32[]{:S(2)}) async-start(bf16[2,64,1024]{2,0,1:T(2,128)(2,1)} %copy.40), calls=%async_computation.1 | async-start | bytes 524288 | tf_op jit(solution)/shard_map/all_to_all | solution.py:49
  112.3 0.0 all-reduce.3.cloned.1.call-start
  112.4 2.3 fusion.17
  114.7 2.0 fusion.14
  116.6 1.1 reshape.59
  117.7 0.8 convolution_bitcast_fusion.1
  118.5 8.8 %all-to-all-done.1 = bf16[2,64,1024]{2,0,1:T(2,128)(2,1)} async-done(((bf16[2,64,1024]{2,0,1:T(2,128)(2,1)}), bf16[2,64,1024]{2,0,1:T(2,128)(2,1)}, u32[]{:S(2)}, u32[]{:S(2)}) %all-to-all-start.1) | async-done | bytes 262176 | tf_op jit(solution)/shard_map/all_to_all | solution.py:49
  127.3 1.0 reshape.57
  128.4 1.8 convolution_bitcast_fusion
  130.2 0.0 all-reduce.3.cloned.1.call-update
  130.2 1.0 convolution_convert_fusion.1
  131.2 1.0 convolution_convert_fusion.3
  132.1 178.1 %all-reduce.3.cloned.1.call-done = (f32[1,128,128]{1,2,0:T(8,128)}, f32[2,64,256]{2,1,0:T(8,128)}, f32[2,256,64]{1,2,0:T(8,128)}, f32[1,128,128]{2,1,0:T(8,128)}) async-done(((f32[1,128,128]{1,2,0:T(8,128)}, f32[2,64,256]{2,1,0:T(8,128)}, f32[2,256,64]{1,2,0:T(8,128)}, f32[1,128,128]{2,1,0:T(8,128)}), (f32[1,128,128]{1,2,0:T(8,128)}, f32[2,64,256]{2,1,0:T(8,128)}, f32[2,256,64]{1,2,0:T(8,128)}, ...) | async-done | bytes 393232 | tf_op jit(solution)/shard_map/psum | solution.py:62
  310.2 1.6 copy.47
  311.8 1.6 copy.80
  313.4 1.6 copy.81
  314.9 1.5 copy.82
  (10 shorter events, 0.0 us)
Async XLA Ops:
  7.2 1.0 copy-start
  7.2 19.0 %copy-start.6 = (bf16[1,128,128]{2,1,0:T(8,128)(2,1)S(1)}, bf16[1,128,128]{2,1,0:T(8,128)(2,1)}, u32[]{:S(2)}) copy-start(bf16[1,128,128]{2,1,0:T(8,128)(2,1)} %param.10) | copy-start | bytes 98308
  7.2 19.0 %copy-start.3 = (bf16[1024,128]{1,0:T(8,128)(2,1)S(1)}, bf16[1024,128]{1,0:T(8,128)(2,1)}, u32[]{:S(2)}) copy-start(bf16[1024,128]{1,0:T(8,128)(2,1)} %param.11) | copy-start | bytes 786436
  11.2 30.0 %all-to-all-start = ((bf16[64,2,1024]{2,1,0:T(2,128)(2,1)}), bf16[64,2,1024]{2,1,0:T(2,128)(2,1)S(1)}, u32[]{:S(2)}, u32[]{:S(2)}) async-start(bf16[64,2,1024]{2,1,0:T(2,128)(2,1)} %reshape.62), calls=%async_computation | async-start | bytes 524288 | tf_op jit(solution)/shard_map/all_to_all | solution.py:47
  41.2 26.2 %all-to-all-start.2 = ((bf16[64,2,1024]{2,1,0:T(2,128)(2,1)}), bf16[64,2,1024]{2,1,0:T(2,128)(2,1)S(1)}, u32[]{:S(2)}, u32[]{:S(2)}) async-start(bf16[64,2,1024]{2,1,0:T(2,128)(2,1)} %reshape.64), calls=%async_computation.2 | async-start | bytes 524288 | tf_op jit(solution)/shard_map/all_to_all | solution.py:52
  52.3 17.6 %copy-start.4 = (bf16[2,64,256]{2,1,0:T(8,128)(2,1)S(1)}, bf16[2,64,256]{2,1,0:T(8,128)(2,1)}, u32[]{:S(2)}) copy-start(bf16[2,64,256]{2,1,0:T(8,128)(2,1)} %param.8) | copy-start | bytes 196612
  69.9 1.6 copy-start.2
  70.0 1.6 copy-start.7
  72.4 1.0 copy-start.1
  74.7 26.3 %all-to-all-start.3 = ((bf16[2,64,1024]{2,0,1:T(2,128)(2,1)}), bf16[2,64,1024]{2,0,1:T(2,128)(2,1)}, u32[]{:S(2)}, u32[]{:S(2)}) async-start(bf16[2,64,1024]{2,0,1:T(2,128)(2,1)} %copy.44), calls=%async_computation.3 | async-start | bytes 524288 | tf_op jit(solution)/shard_map/all_to_all | solution.py:56
  101.0 26.3 %all-to-all-start.1 = ((bf16[2,64,1024]{2,0,1:T(2,128)(2,1)}), bf16[2,64,1024]{2,0,1:T(2,128)(2,1)}, u32[]{:S(2)}, u32[]{:S(2)}) async-start(bf16[2,64,1024]{2,0,1:T(2,128)(2,1)} %copy.40), calls=%async_computation.1 | async-start | bytes 524288 | tf_op jit(solution)/shard_map/all_to_all | solution.py:49
  112.3 197.9 %all-reduce.3.cloned.1.call-start = ((), (), s32[]{:S(2)}) async-start(), calls=%async_computation.4 | async-start | bytes 786432 | tf_op jit(solution)/shard_map/psum | solution.py:62
  116.6 13.6 %copy-start.5 = (bf16[1,128,128]{2,1,0:T(8,128)(2,1)S(1)}, bf16[1,128,128]{2,1,0:T(8,128)(2,1)}, u32[]{:S(2)}) copy-start(bf16[1,128,128]{2,1,0:T(8,128)(2,1)} %param.7) | copy-start | bytes 98308
Sparse Core Ops, SparseCore 0:
  130.3 179.8 all-reduce.2
where the time goes:
time: 324 us; the launch traced here: 323 us
  waiting for transfers between devices  225 us (69%)
  starting transfers between devices  48.7 us (15%)
  local copies, waits for them, and re-layouts  16.3 us (5%)
  between operations  14.2 us (4%)
  matrix products  14.1 us (4%)
  other arithmetic  4.59 us (1%)
    psum x1, waiting for transfers between devices, shards(): lax.psum((grad_u1, grad_u2, grad_d1, grad_d2), 'dp')  178 us
    all_to_all x1, starting transfers between devices, shards(): lax.all_to_all(upper, 'tensor', split_axis=0, concat_axis=1, tiled=True)  14.9 us
    all_to_all x1, waiting for transfers between devices, shards(): lax.all_to_all(upper, 'tensor', split_axis=0, concat_axis=1, tiled=True)  13.2 us
    all_to_all x1, waiting for transfers between devices, shards(): lax.all_to_all(dupper, 'tensor', split_axis=1, concat_axis=0, tiled=True)  12.7 us
    all_to_all x1, waiting for transfers between devices, shards(): lax.all_to_all(dzeta, 'tensor', split_axis=0, concat_axis=1, tiled=True)  12.5 us
    all_to_all x1, starting transfers between devices, shards(): lax.all_to_all(dupper, 'tensor', split_axis=1, concat_axis=0, tiled=True)  11.3 us
    all_to_all x1, starting transfers between devices, shards(): lax.all_to_all(zeta, 'tensor', split_axis=1, concat_axis=0, tiled=True)  11.3 us
    all_to_all x1, starting transfers between devices, shards(): lax.all_to_all(dzeta, 'tensor', split_axis=0, concat_axis=1, tiled=True)  11.1 us
  transfers between devices with their start and end apart: 5, of which 5 were waited for; matrix products, arithmetic and copies ran while one was open for 4% of the time, Pallas kernels for 0%

commit v1 on v0

v1 whole, which is shorter than its diff:
```python
import math

import jax
import jax.numpy as jnp
from jax import lax
from jax.sharding import PartitionSpec as P

F32 = jnp.float32
BF16 = jnp.bfloat16


def mm(spec, a, b, dtype=BF16):
    return jnp.einsum(spec, a, b, preferred_element_type=F32).astype(dtype)


def cdf_part(value):
    return 0.5 * (1.0 + jax.scipy.special.erf(value / math.sqrt(2.0)))


def gelu_deriv(value):
    return cdf_part(value) + value * jnp.exp(-0.5 * value * value) / math.sqrt(2.0 * math.pi)


def row_picks(peers, cols):
    rows = peers * 2 * cols
    row = lax.broadcasted_iota(jnp.int32, (peers * cols, rows), 1)
    unit = lax.broadcasted_iota(jnp.int32, (peers * cols, rows), 0)
    flat = []
    for which in range(2):
        flat.append((row == (unit // cols) * (2 * cols) + which * cols + unit % cols).astype(BF16))
    row = lax.broadcasted_iota(jnp.int32, (cols, peers, rows), 2)
    peer = lax.broadcasted_iota(jnp.int32, (cols, peers, rows), 1)
    col = lax.broadcasted_iota(jnp.int32, (cols, peers, rows), 0)
    grouped = [(row == peer * (2 * cols) + which * cols + col).astype(BF16) for which in range(2)]
    return flat, grouped


def exchange(rows, peers):
    n, t = rows.shape
    out = lax.all_to_all(rows.reshape(peers, n // peers, t), "tensor", split_axis=0, concat_axis=0, tiled=True)
    return out.reshape(n, t)


def group_sum(parts):
    groups = lax.axis_size("dp")
    flat = jnp.concatenate([p.astype(BF16).reshape(groups, -1, 128) for p in parts], axis=1)
    landed = lax.all_to_all(flat, "dp", split_axis=0, concat_axis=0, tiled=True)
    total = jnp.sum(landed.astype(F32), axis=0, keepdims=True).astype(BF16)
    spread = lax.all_to_all(
        jnp.broadcast_to(total, flat.shape), "dp", split_axis=0, concat_axis=0, tiled=True
    )
    out, at = [], 0
    for p in parts:
        n = p.size // groups // 128
        out.append(spread[:, at : at + n].astype(F32).reshape(p.shape))
        at += n
    return out


def shards(tokens, first_up, second_up, first_down, second_down, out_grad):
    peers = lax.axis_size("tensor")
    t = tokens.shape[0]
    cols, _, hidden = second_up.shape
    fu, sd = first_up[0], second_down[0]
    (p0, p1), (q0, q1) = row_picks(peers, cols)

    both = jnp.concatenate([tokens, out_grad], axis=1)
    w_in = jnp.concatenate([mm("jr,ij->ri", p0, fu), mm("jr,jk->rk", p1, sd)], axis=1)
    sent = mm("rc,tc->rt", w_in, both)
    x = exchange(sent, peers)

    w_pre = mm("jbr,jbo->jor", q0, second_up).reshape(cols * hidden, -1)
    w_dact = mm("jbr,job->jor", q1, first_down).reshape(cols * hidden, -1)
    w_z = mm("jbr,job->rjo", q0, first_down).reshape(-1, cols * hidden)
    w_du = mm("jbr,jbo->rjo", q1, second_up).reshape(-1, cols * hidden)
    w_out = jnp.concatenate([mm("jr,jk->rk", p0, sd), mm("jr,ij->ri", p1, fu)], axis=1)

    pre = mm("or,rt->ot", w_pre, x).astype(F32)
    act = (pre * cdf_part(pre)).astype(BF16)
    dact = mm("or,rt->ot", w_dact, x, F32)
    dpre = (dact * gelu_deriv(pre)).astype(BF16)
    back = mm(
        "rc,ct->rt", jnp.concatenate([w_z, w_du], axis=1), jnp.concatenate([act, dpre], axis=0)
    )
    r = exchange(back, peers)

    u_cols = mm("jbr,rt->jbt", q0, x)
    dz_cols = mm("jbr,rt->jbt", q1, x)
    act3 = act.reshape(cols, hidden, t)
    dpre3 = dpre.reshape(cols, hidden, t)
    grad_d1 = mm("jot,jbt->job", act3, dz_cols, F32)
    grad_u2 = mm("jbt,jot->jbo", u_cols, dpre3, F32)

    z_rows = mm("jr,rt->jt", p0, r)
    du_rows = mm("jr,rt->jt", p1, r)
    grad_d2 = mm("jt,tk->jk", z_rows, out_grad, F32)[None]
    grad_u1 = mm("ti,jt->ij", tokens, du_rows, F32)[None]
    outs = mm("rt,rc->tc", r, w_out)
    width = tokens.shape[1]
    g_u1, g_u2, g_d1, g_d2 = group_sum([grad_u1, grad_u2, grad_d1, grad_d2])
    return (outs[:, :width], outs[:, width:], g_u1, g_u2, g_d1, g_d2)


def solution(mesh):
    cols = P("dp", "tensor")
    blocks = P("tensor", None, None)
    return jax.shard_map(
        shards,
        mesh=mesh,
        in_specs=(cols, blocks, blocks, blocks, blocks, cols),
        out_specs=(cols, cols, blocks, blocks, blocks, blocks),
        check_vma=False,
    )
```

time: 324 us -> 150 us (0.46)
  the two profiles are of different devices: /device:TPU:102 before, /device:TPU:35 now
where the time goes in v1:
time: 150 us; the launch traced here: 149 us
  waiting for transfers between devices  89.7 us (60%)
  starting transfers between devices  38.2 us (25%)
  matrix products  11.5 us (8%)
  local copies, waits for them, and re-layouts  6.73 us (4%)
  other arithmetic  2.04 us (1%)
    all_to_all x2, waiting for transfers between devices, exchange(): lax.all_to_all(rows.reshape(peers, n // peers, t), 'tensor', split_axis=0...  52.3 us
    all_to_all x2, starting transfers between devices, exchange(): lax.all_to_all(rows.reshape(peers, n // peers, t), 'tensor', split_axis=0...  24.9 us
    all_to_all x1, waiting for transfers between devices, group_sum(): landed = lax.all_to_all(flat, 'dp', split_axis=0, concat_axis=0, tiled=True)  20.7 us
    all_to_all x1, waiting for transfers between devices, group_sum(): lax.all_to_all(jnp.broadcast_to(total, flat.shape), 'dp', split_axis=0, c...  16.8 us
    dot_general x17, matrix products, mm(): return jnp.einsum(spec, a, b, preferred_element_type=F32).astype(dtype)  11.5 us
    all_to_all x1, starting transfers between devices, group_sum(): landed = lax.all_to_all(flat, 'dp', split_axis=0, concat_axis=0, tiled=True)  9.93 us
    all_to_all x1, starting transfers between devices, group_sum(): lax.all_to_all(jnp.broadcast_to(total, flat.shape), 'dp', split_axis=0, c...  3.39 us
  transfers between devices with their start and end apart: 4, of which 4 were waited for; matrix products, arithmetic and copies ran while one was open for 4% of the time, Pallas kernels for 0%

profile of v1, /device:TPU:35, one launch (start us, length us, event | category | flops | bytes accessed | tf_op | source)
XLA Modules:
  0.0 149.1 jit_solution(12335904401608091864)
XLA Ops:
  0.6 0.0 copy-start
  0.7 1.1 convolution_convert_fusion.12
  1.8 1.1 convolution_convert_fusion.14
  2.9 1.4 convolution_convert_fusion.2
  4.3 0.0 copy-start.2
  4.3 1.0 reshape.89
  5.3 15.9 %all-to-all-start = ((bf16[64,4,1024]{2,1,0:T(4,128)(2,1)}), bf16[64,4,1024]{2,1,0:T(4,128)(2,1)S(1)}, u32[]{:S(2)}, u32[]{:S(2)}) async-start(bf16[64,4,1024]{2,1,0:T(4,128)(2,1)} %reshape.89), calls=%async_computation | async-start | bytes 1048576 | tf_op jit(solution)/shard_map/all_to_all | solution.py:40
  21.3 0.3 convolution_convert_fusion.4
  21.6 0.0 copy-done
  21.6 0.3 convolution_convert_fusion.6
  21.9 0.3 convolution_convert_fusion.3
  22.2 0.3 convolution_convert_fusion.5
  22.5 26.9 %all-to-all-done = bf16[64,4,1024]{2,1,0:T(4,128)(2,1)S(1)} async-done(((bf16[64,4,1024]{2,1,0:T(4,128)(2,1)}), bf16[64,4,1024]{2,1,0:T(4,128)(2,1)S(1)}, u32[]{:S(2)}, u32[]{:S(2)}) %all-to-all-start) | async-done | bytes 524320 | tf_op jit(solution)/shard_map/all_to_all | solution.py:40
  49.4 0.1 reshape.90
  49.5 0.6 fusion.3
  50.1 1.0 fusion.8
  51.1 1.0 copy-done.1
  52.1 0.7 fusion.13
  52.8 1.0 reshape.92
  53.9 8.9 %all-to-all-start.1 = ((bf16[64,4,1024]{2,1,0:T(4,128)(2,1)}), bf16[64,4,1024]{2,1,0:T(4,128)(2,1)S(1)}, u32[]{:S(2)}, u32[]{:S(2)}) async-start(bf16[64,4,1024]{2,1,0:T(4,128)(2,1)} %reshape.92), calls=%async_computation.1 | async-start | bytes 1048576 | tf_op jit(solution)/shard_map/all_to_all | solution.py:40
  62.8 0.1 reshape.116
  62.9 1.8 %fusion.21 = bf16[2,64,256]{2,1,0:T(8,128)(2,1)S(1)} fusion(bf16[2,256,1024]{2,1,0:T(8,128)(2,1)} %bitcast.54, bf16[256,1024,1]{1,0,2:T(8,128)(2,1)S(1)} %reshape.116, s32[64]{0:T(128)S(1)} %iota_multiply_fusion), kind=kOutput, calls=%fused_computation.35 | convolution fusion | flops 134447104 | bytes 1638656 | tf_op jit(solution)/shard_map/jbt,jot->jbo/dot_general | solution.py:13
  64.7 0.6 fusion.20
  65.3 0.0 copy-start.3
  65.3 0.1 copy.12
  65.5 0.1 reshape.98
  65.6 0.0 copy-start.4
  65.6 25.3 %all-to-all-done.1 = bf16[64,4,1024]{2,1,0:T(4,128)(2,1)S(1)} async-done(((bf16[64,4,1024]{2,1,0:T(4,128)(2,1)}), bf16[64,4,1024]{2,1,0:T(4,128)(2,1)S(1)}, u32[]{:S(2)}, u32[]{:S(2)}) %all-to-all-start.1) | async-done | bytes 524320 | tf_op jit(solution)/shard_map/all_to_all | solution.py:40
  90.9 0.1 reshape.93
  91.1 0.5 fusion.23
  91.6 0.0 copy-start.5
  91.6 0.4 fusion.22
  92.1 0.0 copy-start.6
  92.1 0.7 pad_maximum_fusion
  92.8 9.9 %all-to-all-start.2 = ((bf16[8,96,128]{2,1,0:T(8,128)(2,1)}), bf16[8,96,128]{2,1,0:T(8,128)(2,1)S(1)}, u32[]{:S(2)}, u32[]{:S(2)}) async-start(bf16[8,96,128]{2,1,0:T(8,128)(2,1)} %pad_maximum_fusion), calls=%async_computation.2 | async-start | bytes 393216 | tf_op jit(solution)/shard_map/all_to_all | solution.py:47
  102.7 0.3 convolution_convert_fusion.11
  103.1 20.7 %all-to-all-done.2 = bf16[8,96,128]{2,1,0:T(8,128)(2,1)S(1)} async-done(((bf16[8,96,128]{2,1,0:T(8,128)(2,1)}), bf16[8,96,128]{2,1,0:T(8,128)(2,1)S(1)}, u32[]{:S(2)}, u32[]{:S(2)}) %all-to-all-start.2) | async-done | bytes 196640 | tf_op jit(solution)/shard_map/all_to_all | solution.py:47
  123.8 0.7 broadcast_in_dim.2
  124.5 3.4 %all-to-all-start.3 = ((bf16[8,96,128]{2,1,0:T(8,128)(2,1)}), bf16[8,96,128]{2,1,0:T(8,128)(2,1)S(1)}, u32[]{:S(2)}, u32[]{:S(2)}) async-start(bf16[8,96,128]{2,1,0:T(8,128)(2,1)} %broadcast_in_dim.2), calls=%async_computation.3 | async-start | bytes 393216 | tf_op jit(solution)/shard_map/all_to_all | solution.py:49
  127.9 0.4 convolution_convert_fusion.13
  128.3 0.4 convolution_convert_fusion.1
  128.6 0.8 fusion.63
  129.5 16.8 %all-to-all-done.3 = bf16[8,96,128]{2,1,0:T(8,128)(2,1)S(1)} async-done(((bf16[8,96,128]{2,1,0:T(8,128)(2,1)}), bf16[8,96,128]{2,1,0:T(8,128)(2,1)S(1)}, u32[]{:S(2)}, u32[]{:S(2)}) %all-to-all-start.3) | async-done | bytes 196640 | tf_op jit(solution)/shard_map/all_to_all | solution.py:49
  146.3 0.1 reshape.113
  146.4 0.8 copy.13
  147.1 0.7 reshape.111
  147.8 0.6 bitcast_convert_fusion
  148.5 0.6 bitcast_convert_fusion.1
  (15 shorter events, 0.1 us)
Async XLA Ops:
  0.6 20.9 %copy-start = (bf16[2,256,64]{1,2,0:T(8,128)(2,1)S(1)}, bf16[2,256,64]{1,2,0:T(8,128)(2,1)}, u32[]{:S(2)}) copy-start(bf16[2,256,64]{1,2,0:T(8,128)(2,1)} %param.9) | copy-start | bytes 196612
  4.3 17.0 %copy-start.2 = (bf16[2,64,256]{2,1,0:T(8,128)(2,1)S(1)}, bf16[2,64,256]{2,1,0:T(8,128)(2,1)}, u32[]{:S(2)}) copy-start(bf16[2,64,256]{2,1,0:T(8,128)(2,1)} %param.8) | copy-start | bytes 196612
  5.3 44.1 %all-to-all-start = ((bf16[64,4,1024]{2,1,0:T(4,128)(2,1)}), bf16[64,4,1024]{2,1,0:T(4,128)(2,1)S(1)}, u32[]{:S(2)}, u32[]{:S(2)}) async-start(bf16[64,4,1024]{2,1,0:T(4,128)(2,1)} %reshape.89), calls=%async_computation | async-start | bytes 1048576 | tf_op jit(solution)/shard_map/all_to_all | solution.py:40
  51.1 1.0 copy-start.1
  53.9 37.1 %all-to-all-start.1 = ((bf16[64,4,1024]{2,1,0:T(4,128)(2,1)}), bf16[64,4,1024]{2,1,0:T(4,128)(2,1)S(1)}, u32[]{:S(2)}, u32[]{:S(2)}) async-start(bf16[64,4,1024]{2,1,0:T(4,128)(2,1)} %reshape.92), calls=%async_computation.1 | async-start | bytes 1048576 | tf_op jit(solution)/shard_map/all_to_all | solution.py:40
  65.3 25.7 %copy-start.3 = (bf16[1024,128]{1,0:T(8,128)(2,1)S(1)}, bf16[1024,128]{1,0:T(8,128)(2,1)}, u32[]{:S(2)}) copy-start(bf16[1024,128]{1,0:T(8,128)(2,1)} %param.6) | copy-start | bytes 786436
  65.6 26.0 %copy-start.4 = (bf16[1024,128]{1,0:T(8,128)(2,1)S(1)}, bf16[1024,128]{1,0:T(8,128)(2,1)}, u32[]{:S(2)}) copy-start(bf16[1024,128]{1,0:T(8,128)(2,1)} %param.11) | copy-start | bytes 786436
  91.6 11.1 %copy-start.5 = (bf16[1,128,128]{2,1,0:T(8,128)(2,1)S(1)}, bf16[1,128,128]{2,1,0:T(8,128)(2,1)}, u32[]{:S(2)}) copy-start(bf16[1,128,128]{2,1,0:T(8,128)(2,1)} %param.7) | copy-start | bytes 98308
  92.1 35.8 %copy-start.6 = (bf16[1,128,128]{2,1,0:T(8,128)(2,1)S(1)}, bf16[1,128,128]{2,1,0:T(8,128)(2,1)}, u32[]{:S(2)}) copy-start(bf16[1,128,128]{2,1,0:T(8,128)(2,1)} %param.10) | copy-start | bytes 98308
  92.8 31.0 %all-to-all-start.2 = ((bf16[8,96,128]{2,1,0:T(8,128)(2,1)}), bf16[8,96,128]{2,1,0:T(8,128)(2,1)S(1)}, u32[]{:S(2)}, u32[]{:S(2)}) async-start(bf16[8,96,128]{2,1,0:T(8,128)(2,1)} %pad_maximum_fusion), calls=%async_computation.2 | async-start | bytes 393216 | tf_op jit(solution)/shard_map/all_to_all | solution.py:47
  124.5 21.7 %all-to-all-start.3 = ((bf16[8,96,128]{2,1,0:T(8,128)(2,1)}), bf16[8,96,128]{2,1,0:T(8,128)(2,1)S(1)}, u32[]{:S(2)}, u32[]{:S(2)}) async-start(bf16[8,96,128]{2,1,0:T(8,128)(2,1)} %broadcast_in_dim.2), calls=%async_computation.3 | async-start | bytes 393216 | tf_op jit(solution)/shard_map/all_to_all | solution.py:49

commit v2 on v1

v2 whole, which is shorter than its diff:
```python
import functools
import math

import jax
import jax.numpy as jnp
from jax import lax
from jax.experimental import pallas as pl
from jax.experimental.pallas import tpu as pltpu
from jax.sharding import PartitionSpec as P

F32 = jnp.float32
BF16 = jnp.bfloat16


def mm(spec, a, b, dtype=BF16):
    return jnp.einsum(spec, a, b, preferred_element_type=F32).astype(dtype)


def cdf_part(value):
    return 0.5 * (1.0 + jax.scipy.special.erf(value / math.sqrt(2.0)))


def gelu_deriv(value):
    return cdf_part(value) + value * jnp.exp(-0.5 * value * value) / math.sqrt(2.0 * math.pi)


def row_picks(peers, cols):
    rows = peers * 2 * cols
    row = lax.broadcasted_iota(jnp.int32, (peers * cols, rows), 1)
    unit = lax.broadcasted_iota(jnp.int32, (peers * cols, rows), 0)
    flat = []
    for which in range(2):
        flat.append((row == (unit // cols) * (2 * cols) + which * cols + unit % cols).astype(BF16))
    row = lax.broadcasted_iota(jnp.int32, (cols, peers, rows), 2)
    peer = lax.broadcasted_iota(jnp.int32, (cols, peers, rows), 1)
    col = lax.broadcasted_iota(jnp.int32, (cols, peers, rows), 0)
    grouped = [(row == peer * (2 * cols) + which * cols + col).astype(BF16) for which in range(2)]
    return flat, grouped


def greet(axis_sizes):
    barrier = pltpu.get_barrier_semaphore()
    for axis, n in axis_sizes:
        me = lax.axis_index(axis)

        def tell(k, carry, axis=axis, n=n, me=me):
            pl.semaphore_signal(
                barrier, inc=1, device_id={axis: (me + k) % n}, device_id_type=pl.DeviceIdType.MESH
            )
            return carry

        lax.fori_loop(1, n, tell, 0)


def greeted(axis_sizes):
    pl.semaphore_wait(pltpu.get_barrier_semaphore(), sum(n - 1 for _, n in axis_sizes))


def remote(src, dst, send, recv, axis, peer):
    return pltpu.make_async_remote_copy(
        src_ref=src,
        dst_ref=dst,
        send_sem=send,
        recv_sem=recv,
        device_id={axis: peer},
        device_id_type=pl.DeviceIdType.MESH,
    )


def start_exchange(src, dst, sems, n):
    me = lax.axis_index("tensor")

    def push(i, carry):
        step = (i % 8 // 2) * (n // 4) + ((i // 8 + n // 16) % (n // 8)) * 2 + i % 2
        peer = (me + step) % n
        remote(src.at[peer], dst.at[me], sems.at[0], sems.at[1], "tensor", peer).start()
        return carry

    lax.fori_loop(0, n // 2, push, 0)
    lax.fori_loop(n // 2 + 1, n, push, 0)
    own = pltpu.make_async_copy(src.at[me], dst.at[me], sems.at[2])
    own.start()
    return own


def end_exchange(src, dst, sems, n, own):
    own.wait()
    span = pl.ds(0, n - 1)
    all_of = remote(src.at[span], dst.at[span], sems.at[0], sems.at[1], "tensor", 0)
    all_of.wait_recv()
    all_of.wait_send()


def sum_scatter(flat, land, sems, n):
    me = lax.axis_index("dp")

    def push(k, carry):
        peer = (me + k) % n
        remote(flat.at[peer], land.at[me], sems.at[0], sems.at[1], "dp", peer).start()
        return carry

    lax.fori_loop(1, n, push, 0)
    land[pl.ds(me, 1)] = flat[pl.ds(me, 1)]


def sum_spread(flat, land, total, gath, sems, n):
    me = lax.axis_index("dp")
    span = pl.ds(0, n - 1)
    first = remote(flat.at[span], land.at[span], sems.at[0], sems.at[1], "dp", 0)
    first.wait_recv()
    acc = land[0].astype(F32)
    for k in range(1, n):
        acc = acc + land[k].astype(F32)
    total[...] = acc.astype(BF16)
    gath[pl.ds(me, 1)] = acc.astype(BF16)[None]

    def push(k, carry):
        peer = (me + k) % n
        remote(total, gath.at[me], sems.at[2], sems.at[3], "dp", peer).start()
        return carry

    lax.fori_loop(1, n, push, 0)
    first.wait_send()


def sum_end(gath, sems, n):
    span = pl.ds(0, n - 1)
    last = remote(gath.at[span], gath.at[span], sems.at[2], sems.at[3], "dp", 0)
    last.wait_recv()
    last.wait_send()


def dot_nt(a, b):
    return lax.dot_general(a, b, (((1,), (1,)), ((), ())), preferred_element_type=F32)


def dot(a, b):
    return jnp.dot(a, b, preferred_element_type=F32)


def first_kernel(n, src, dst, sems):
    greet((("tensor", n),))
    greeted((("tensor", n),))
    own = start_exchange(src, dst, sems, n)
    end_exchange(src, dst, sems, n, own)


def middle_kernel(n, g, src, x, act, dpre, q0, q1, dst, out, flat, land, total, gath, sems, dsems):
    axes = (("tensor", n), ("dp", g))
    cols = q0.shape[0]
    rows, width = flat.shape[2:]
    greet(axes)
    for j in range(cols):
        u = dot(q0[j], x[...]).astype(BF16)
        dz = dot(q1[j], x[...]).astype(BF16)
        flat[:, j] = dot_nt(u, dpre[j]).reshape(g, rows, width).astype(BF16)
        flat[:, cols + j] = dot_nt(dz, act[j]).reshape(g, rows, width).astype(BF16)
    greeted(axes)
    sum_scatter(flat, land, dsems, g)
    own = start_exchange(src, dst, sems, n)
    sum_spread(flat, land, total, gath, dsems, g)
    sum_end(gath, dsems, g)
    for m in range(2 * cols):
        out[m] = gath[:, m].astype(F32).reshape(g * rows, width)
    end_exchange(src, dst, sems, n, own)


def last_kernel(g, r, tok, og, p0, p1, out, flat, land, total, gath, dsems):
    axes = (("dp", g),)
    rows, width = flat.shape[2:]
    greet(axes)
    z = dot(p0[...], r[...]).astype(BF16)
    flat[:, 0] = dot(z, og[...]).reshape(g, rows, width).astype(BF16)
    du = dot(p1[...], r[...]).astype(BF16)
    flat[:, 1] = dot(du, tok[...]).T.reshape(g, rows, width).astype(BF16)
    greeted(axes)
    sum_scatter(flat, land, dsems, g)
    sum_spread(flat, land, total, gath, dsems, g)
    sum_end(gath, dsems, g)
    for m in range(2):
        out[m] = gath[:, m].astype(F32).reshape(g * rows, width)


def sum_scratch(g, mats, rows, width):
    return [
        pltpu.VMEM((g, mats, rows, width), BF16),
        pltpu.VMEM((g, mats, rows, width), BF16),
        pltpu.VMEM((mats, rows, width), BF16),
        pltpu.VMEM((g, mats, rows, width), BF16),
    ]


def kernel_call(body, ins, outs, scratch, ident):
    vmem = pl.BlockSpec(memory_space=pltpu.VMEM)
    return pl.pallas_call(
        body,
        out_shape=outs,
        in_specs=[vmem] * len(ins),
        out_specs=[vmem] * len(outs),
        scratch_shapes=scratch,
        compiler_params=pltpu.CompilerParams(collective_id=ident, has_side_effects=True),
    )(*ins)


def shards(tokens, first_up, second_up, first_down, second_down, out_grad):
    peers = lax.axis_size("tensor")
    t = tokens.shape[0]
    cols, _, hidden = second_up.shape
    fu, sd = first_up[0], second_down[0]
    (p0, p1), (q0, q1) = row_picks(peers, cols)

    both = jnp.concatenate([tokens, out_grad], axis=1)
    w_in = jnp.concatenate([mm("jr,ij->ri", p0, fu), mm("jr,jk->rk", p1, sd)], axis=1)
    sent = mm("rc,tc->rt", w_in, both)
    groups = lax.axis_size("dp")
    block = jax.ShapeDtypeStruct((peers, 2 * cols, t), BF16)
    links = pltpu.SemaphoreType.DMA((3,))
    sums = pltpu.SemaphoreType.DMA((4,))
    (x,) = kernel_call(
        functools.partial(first_kernel, peers), [sent.reshape(block.shape)], [block], [links], 0
    )
    x = x.reshape(sent.shape)

    w_pre = mm("jbr,jbo->jor", q0, second_up).reshape(cols * hidden, -1)
    w_dact = mm("jbr,job->jor", q1, first_down).reshape(cols * hidden, -1)
    w_z = mm("jbr,job->rjo", q0, first_down).reshape(-1, cols * hidden)
    w_du = mm("jbr,jbo->rjo", q1, second_up).reshape(-1, cols * hidden)
    w_out = jnp.concatenate([mm("jr,jk->rk", p0, sd), mm("jr,ij->ri", p1, fu)], axis=1)

    pre = mm("or,rt->ot", w_pre, x).astype(F32)
    act = (pre * cdf_part(pre)).astype(BF16)
    dact = mm("or,rt->ot", w_dact, x, F32)
    dpre = (dact * gelu_deriv(pre)).astype(BF16)
    back = mm(
        "rc,ct->rt", jnp.concatenate([w_z, w_du], axis=1), jnp.concatenate([act, dpre], axis=0)
    )
    r, mids = kernel_call(
        functools.partial(middle_kernel, peers, groups),
        [
            back.reshape(block.shape),
            x,
            act.reshape(cols, hidden, t),
            dpre.reshape(cols, hidden, t),
            q0,
            q1,
        ],
        [block, jax.ShapeDtypeStruct((2 * cols, peers, hidden), F32)],
        sum_scratch(groups, 2 * cols, peers // groups, hidden) + [links, sums],
        1,
    )
    r = r.reshape(sent.shape)
    width = tokens.shape[1]
    (ends,) = kernel_call(
        functools.partial(last_kernel, groups),
        [r, tokens, out_grad, p0, p1],
        [jax.ShapeDtypeStruct((2, width, width), F32)],
        sum_scratch(groups, 2, width // groups, width) + [sums],
        2,
    )
    outs = mm("rt,rc->tc", r, w_out)
    return (
        outs[:, :width],
        outs[:, width:],
        ends[1:],
        mids[:cols],
        mids[cols:].swapaxes(1, 2),
        ends[:1],
    )


def solution(mesh):
    cols = P("dp", "tensor")
    blocks = P("tensor", None, None)
    return jax.shard_map(
        shards,
        mesh=mesh,
        in_specs=(cols, blocks, blocks, blocks, blocks, cols),
        out_specs=(cols, cols, blocks, blocks, blocks, blocks),
        check_vma=False,
    )
```

time: 150 us -> 135 us (0.900)
  the two profiles are of different devices: /device:TPU:35 before, /device:TPU:64 now
where the time goes in v2:
time: 135 us; the launch traced here: 134 us
  Pallas kernels  116 us (86%)
  matrix products  8.16 us (6%)
  local copies, waits for them, and re-layouts  7.44 us (6%)
  other arithmetic  1.59 us (1%)
    pallas_call x3, Pallas kernels, kernel_call(): pl.pallas_call(body, out_shape=outs, in_specs=[vmem] * len(ins), out_spec...  116 us
    dot_general x13, matrix products, mm(): return jnp.einsum(spec, a, b, preferred_element_type=F32).astype(dtype)  8.16 us

profile of v2, /device:TPU:64, one launch (start us, length us, event | category | flops | bytes accessed | tf_op | source)
XLA Modules:
  0.0 134.3 jit_solution(11615844978016984023)
XLA Ops:
  0.6 0.0 copy-start
  0.7 1.1 convolution_convert_fusion.10
  1.8 1.1 convolution_convert_fusion.8
  2.9 1.4 %convolution_convert_fusion.2 = bf16[256,1024]{1,0:T(8,128)(2,1)S(1)} fusion(bf16[1024,128]{1,0:T(8,128)(2,1)} %og.1, bf16[1024,128]{1,0:T(8,128)(2,1)} %tok.1, bf16[256,128]{1,0:T(8,128)(2,1)S(1)} %convolution_convert_fusion.10, bf16[256,128]{1,0:T(8,128)(2,1)S(1)} %convolution_convert_fusion.8), kind=kOutput, calls=%fused_computation.20 | convolution fusion | flops 135790592 | bytes 1179648 | tf_op jit(solution)/shard_map/rc,tc->rt/dot_general | solution.py:16
  4.3 1.0 reshape.45.src
  5.3 0.0 copy-start.5
  5.3 35.4 %shard_map.109 = bf16[64,4,1024]{2,1,0:T(4,128)(2,1)} custom-call(bf16[64,4,1024]{2,1,0:T(4,128)(2,1)} %reshape.45.src), custom_call_target="tpu_custom_call" | custom-call | tf_op jit(solution)/shard_map/pallas_call | solution.py:195
  40.7 1.2 reshape.46.x
  41.9 0.0 copy-start.2
  41.9 0.0 copy-done.5
  41.9 0.3 convolution_convert_fusion.4
  42.2 0.6 fusion.3
  42.8 0.0 copy-start.3
  42.8 0.0 copy-done
  42.8 0.3 convolution_convert_fusion.3
  43.1 0.0 copy-done.2
  43.1 1.0 fusion.8
  44.2 0.0 copy-start.4
  44.2 0.3 convolution_convert_fusion.6
  44.5 0.3 convolution_convert_fusion.5
  44.8 0.0 copy-done.3
  44.8 0.7 fusion.13
  45.5 0.0 copy-done.4
  45.5 1.0 reshape.48.src
  46.5 0.7 fusion.30
  47.3 55.0 %shard_map.110 = (bf16[64,4,1024]{2,1,0:T(4,128)(2,1)}, f32[4,64,256]{2,1,0:T(8,128)}) custom-call(bf16[64,4,1024]{2,1,0:T(4,128)(2,1)} %reshape.48.src, bf16[256,1024]{1,0:T(8,128)(2,1)} %copy-done.2, bf16[2,256,1024]{2,1,0:T(8,128)(2,1)} %bitcast.35, bf16[2,256,1024]{2,1,0:T(8,128)(2,1)} %bitcast.36, bf16[2,64,256]{2,1,0:T(8,128)(2,1)} %get-tuple-element.27.q0, ...), custom_call_target="tpu_custom_call" | custom-call | tf_op jit(solution)/shard_map/pallas_call | solution.py:195
  102.2 0.0 copy-start.7
  102.3 0.0 copy-start.8
  102.3 1.2 reshape.51.r
  103.4 0.0 copy-done.7
  103.4 0.0 copy-start.1
  103.5 0.3 convolution_convert_fusion.7
  103.8 0.0 copy-done.8
  103.8 0.4 convolution_convert_fusion.9
  104.2 0.4 convolution_convert_fusion.1
  104.5 0.8 fusion.51
  105.4 0.0 copy-done.1
  105.4 0.0 copy-start.6
  105.4 0.8 fusion.46
  106.2 25.8 %shard_map.111 = f32[2,128,128]{2,1,0:T(8,128)} custom-call(bf16[256,1024]{1,0:T(8,128)(2,1)} %copy-done.1, bf16[1024,128]{1,0:T(8,128)(2,1)} %tok.1, bf16[1024,128]{1,0:T(8,128)(2,1)} %og.1, bf16[128,256]{1,0:T(8,128)(2,1)} %get-tuple-element.17.p0, bf16[128,256]{1,0:T(8,128)(2,1)} %get-tuple-element.16.p1), custom_call_target="tpu_custom_call" | custom-call | tf_op jit(solution)/shard_map/pallas_call | solution.py:195
  132.0 1.5 %fusion.52 = (f32[1,128,128]{2,1,0:T(8,128)}, f32[1,128,128]{2,1,0:T(8,128)}) fusion(f32[2,128,128]{2,1,0:T(8,128)} %shard_map.111), kind=kLoop, calls=%fused_computation.77 | loop fusion | bytes 262144 | tf_op jit(solution)/shard_map/slice | solution.py:267
  133.6 0.0 copy-done.6
  133.6 0.7 slice_bitcast_fusion
  (5 shorter events, 0.0 us)
Async XLA Ops:
  0.6 42.2 %copy-start = (bf16[2,256,64]{1,2,0:T(8,128)(2,1)S(1)}, bf16[2,256,64]{1,2,0:T(8,128)(2,1)}, u32[]{:S(2)}) copy-start(bf16[2,256,64]{1,2,0:T(8,128)(2,1)} %param.9) | copy-start | bytes 196612
  5.3 36.6 %copy-start.5 = (bf16[2,64,256]{2,1,0:T(8,128)(2,1)S(1)}, bf16[2,64,256]{2,1,0:T(8,128)(2,1)}, u32[]{:S(2)}) copy-start(bf16[2,64,256]{2,1,0:T(8,128)(2,1)} %param.8) | copy-start | bytes 196612
  41.9 1.3 copy-start.2
  42.8 2.0 %copy-start.3 = (bf16[512,1024]{1,0:T(8,128)(2,1)}, bf16[512,1024]{1,0:T(8,128)(2,1)S(1)}, u32[]{:S(2)}) copy-start(bf16[512,1024]{1,0:T(8,128)(2,1)S(1)} %get-tuple-element.18) | copy-start | bytes 3145732
  44.2 1.4 %copy-start.4 = (bf16[512,1024]{1,0:T(8,128)(2,1)}, bf16[512,1024]{1,0:T(8,128)(2,1)S(1)}, u32[]{:S(2)}) copy-start(bf16[512,1024]{1,0:T(8,128)(2,1)S(1)} %fusion.8) | copy-start | bytes 3145732
  102.2 1.2 copy-start.7
  102.3 1.6 %copy-start.8 = (bf16[1,128,128]{2,1,0:T(8,128)(2,1)S(1)}, bf16[1,128,128]{2,1,0:T(8,128)(2,1)}, u32[]{:S(2)}) copy-start(bf16[1,128,128]{2,1,0:T(8,128)(2,1)} %param.10) | copy-start | bytes 98308
  103.4 1.9 %copy-start.1 = (bf16[256,1024]{1,0:T(8,128)(2,1)}, bf16[256,1024]{1,0:T(8,128)(2,1)S(1)}, u32[]{:S(2)}) copy-start(bf16[256,1024]{1,0:T(8,128)(2,1)S(1)} %reshape.51.r) | copy-start | bytes 1572868
  105.4 28.2 %copy-start.6 = (f32[4,64,256]{2,1,0:T(8,128)S(1)}, f32[4,64,256]{2,1,0:T(8,128)}, u32[]{:S(2)}) copy-start(f32[4,64,256]{2,1,0:T(8,128)} %get-tuple-element.9) | copy-start | bytes 786436

commit v3 on v2

--- a/solution.py
+++ b/solution.py
@@ -67,7 +67,7 @@
     )
 
 
-def start_exchange(src, dst, sems, n):
+def start_exchange(src, dst, sems, n, spans):
     me = lax.axis_index("tensor")
 
     def push(i, carry):
@@ -76,57 +76,74 @@
         remote(src.at[peer], dst.at[me], sems.at[0], sems.at[1], "tensor", peer).start()
         return carry
 
-    lax.fori_loop(0, n // 2, push, 0)
-    lax.fori_loop(n // 2 + 1, n, push, 0)
-    own = pltpu.make_async_copy(src.at[me], dst.at[me], sems.at[2])
-    own.start()
-    return own
-
-
-def end_exchange(src, dst, sems, n, own):
-    own.wait()
+    for lo, hi in spans:
+        lax.fori_loop(lo, hi, push, 0)
+
+
+def keep_own(src, dst, sems):
+    me = lax.axis_index("tensor")
+    return pltpu.make_async_copy(src.at[me], dst.at[me], sems.at[2])
+
+
+def end_exchange(src, dst, sems, n):
+    keep_own(src, dst, sems).wait()
     span = pl.ds(0, n - 1)
     all_of = remote(src.at[span], dst.at[span], sems.at[0], sems.at[1], "tensor", 0)
     all_of.wait_recv()
     all_of.wait_send()
 
 
-def sum_scatter(flat, land, sems, n):
+def sum_scatter(flat, land, sems, ny):
     me = lax.axis_index("dp")
+    y, half = me // 2, me % 2
 
     def push(k, carry):
-        peer = (me + k) % n
-        remote(flat.at[peer], land.at[me], sems.at[0], sems.at[1], "dp", peer).start()
+        peer = (y + k) % ny
+        remote(flat.at[peer], land.at[y], sems.at[0], sems.at[1], "dp", peer * 2 + half).start()
         return carry
 
-    lax.fori_loop(1, n, push, 0)
-    land[pl.ds(me, 1)] = flat[pl.ds(me, 1)]
-
-
-def sum_spread(flat, land, total, gath, sems, n):
+    lax.fori_loop(1, ny, push, 0)
+    land[pl.ds(y, 1)] = flat[pl.ds(y, 1)]
+
+
+def sum_swap(flat, land, pair, sems, ny):
     me = lax.axis_index("dp")
-    span = pl.ds(0, n - 1)
+    span = pl.ds(0, ny - 1)
     first = remote(flat.at[span], land.at[span], sems.at[0], sems.at[1], "dp", 0)
     first.wait_recv()
     acc = land[0].astype(F32)
-    for k in range(1, n):
+    for k in range(1, ny):
         acc = acc + land[k].astype(F32)
-    total[...] = acc.astype(BF16)
-    gath[pl.ds(me, 1)] = acc.astype(BF16)[None]
+    pair[0] = acc.astype(BF16)
+    other = me // 2 * 2 + (1 - me % 2)
+    remote(pair.at[0], pair.at[1], sems.at[2], sems.at[3], "dp", other).start()
+    first.wait_send()
+
+
+def sum_spread(pair, total, gath, sems, ny):
+    me = lax.axis_index("dp")
+    y, half = me // 2, me % 2
+    swap = remote(pair.at[0], pair.at[1], sems.at[2], sems.at[3], "dp", 0)
+    swap.wait_recv()
+    acc = (pair[0].astype(F32) + pair[1].astype(F32)).astype(BF16)
+    total[...] = acc
+    gath[pl.ds(y, 1)] = acc[None]
 
     def push(k, carry):
-        peer = (me + k) % n
-        remote(total, gath.at[me], sems.at[2], sems.at[3], "dp", peer).start()
+        peer = (y + k) % ny
+        remote(total, gath.at[y], sems.at[4], sems.at[5], "dp", peer * 2 + half).start()
         return carry
 
-    lax.fori_loop(1, n, push, 0)
-    first.wait_send()
-
-
-def sum_end(gath, sems, n):
-    span = pl.ds(0, n - 1)
-    last = remote(gath.at[span], gath.at[span], sems.at[2], sems.at[3], "dp", 0)
+    lax.fori_loop(1, ny, push, 0)
+    swap.wait_send()
+
+
+def sum_end(gath, out, sems, ny):
+    span = pl.ds(0, ny - 1)
+    last = remote(gath.at[span], gath.at[span], sems.at[4], sems.at[5], "dp", 0)
     last.wait_recv()
+    for m in range(out.shape[0]):
+        out[m] = gath[:, m].astype(F32).reshape(out.shape[1:])
     last.wait_send()
 
 
@@ -136,57 +153,66 @@
 
 def dot(a, b):
     return jnp.dot(a, b, preferred_element_type=F32)
+
+
+def dot_tn(a, b):
+    return lax.dot_general(a, b, (((0,), (0,)), ((), ())), preferred_element_type=F32)
 
 
 def first_kernel(n, src, dst, sems):
     greet((("tensor", n),))
     greeted((("tensor", n),))
-    own = start_exchange(src, dst, sems, n)
-    end_exchange(src, dst, sems, n, own)
-
-
-def middle_kernel(n, g, src, x, act, dpre, q0, q1, dst, out, flat, land, total, gath, sems, dsems):
+    start_exchange(src, dst, sems, n, ((0, n // 2), (n // 2 + 1, n)))
+    keep_own(src, dst, sems).start()
+    end_exchange(src, dst, sems, n)
+
+
+def rest_kernel(
+    n, g, src, x, act, dpre, q0, q1, tok, og, p0, p1, w_out,
+    output, tok_grad, mids, ends,
+    dst, flat, land, pair, total, gath, flat2, land2, pair2, total2, gath2, links, sums, sums2,
+):
     axes = (("tensor", n), ("dp", g))
+    ny = g // 2
     cols = q0.shape[0]
-    rows, width = flat.shape[2:]
+    rows, hidden = flat.shape[2:]
+    width = tok.shape[1]
     greet(axes)
     for j in range(cols):
         u = dot(q0[j], x[...]).astype(BF16)
         dz = dot(q1[j], x[...]).astype(BF16)
-        flat[:, j] = dot_nt(u, dpre[j]).reshape(g, rows, width).astype(BF16)
-        flat[:, cols + j] = dot_nt(dz, act[j]).reshape(g, rows, width).astype(BF16)
+        flat[:, j] = dot_nt(u, dpre[j]).reshape(ny, rows, hidden).astype(BF16)
+        flat[:, cols + j] = dot_nt(dz, act[j]).reshape(ny, rows, hidden).astype(BF16)
     greeted(axes)
-    sum_scatter(flat, land, dsems, g)
-    own = start_exchange(src, dst, sems, n)
-    sum_spread(flat, land, total, gath, dsems, g)
-    sum_end(gath, dsems, g)
-    for m in range(2 * cols):
-        out[m] = gath[:, m].astype(F32).reshape(g * rows, width)
-    end_exchange(src, dst, sems, n, own)
-
-
-def last_kernel(g, r, tok, og, p0, p1, out, flat, land, total, gath, dsems):
-    axes = (("dp", g),)
-    rows, width = flat.shape[2:]
-    greet(axes)
-    z = dot(p0[...], r[...]).astype(BF16)
-    flat[:, 0] = dot(z, og[...]).reshape(g, rows, width).astype(BF16)
-    du = dot(p1[...], r[...]).astype(BF16)
-    flat[:, 1] = dot(du, tok[...]).T.reshape(g, rows, width).astype(BF16)
-    greeted(axes)
-    sum_scatter(flat, land, dsems, g)
-    sum_spread(flat, land, total, gath, dsems, g)
-    sum_end(gath, dsems, g)
-    for m in range(2):
-        out[m] = gath[:, m].astype(F32).reshape(g * rows, width)
-
-
-def sum_scratch(g, mats, rows, width):
+    sum_scatter(flat, land, sums, ny)
+    start_exchange(src, dst, links, n, ((0, n // 4), (n // 2 + 1, n)))
+    keep_own(src, dst, links).start()
+    sum_swap(flat, land, pair, sums, ny)
+    start_exchange(src, dst, links, n, ((n // 4, n // 2),))
+    sum_spread(pair, total, gath, sums, ny)
+    sum_end(gath, mids, sums, ny)
+    end_exchange(src, dst, links, n)
+
+    r = dst[...].reshape(n * dst.shape[1], dst.shape[2])
+    z = dot(p0[...], r).astype(BF16)
+    flat2[:, 0] = dot(z, og[...]).reshape(ny, width // ny, width).astype(BF16)
+    du = dot(p1[...], r).astype(BF16)
+    flat2[:, 1] = dot(du, tok[...]).T.reshape(ny, width // ny, width).astype(BF16)
+    sum_scatter(flat2, land2, sums2, ny)
+    output[...] = dot_tn(r, w_out[:, :width]).astype(BF16)
+    sum_swap(flat2, land2, pair2, sums2, ny)
+    tok_grad[...] = dot_tn(r, w_out[:, width:]).astype(BF16)
+    sum_spread(pair2, total2, gath2, sums2, ny)
+    sum_end(gath2, ends, sums2, ny)
+
+
+def sum_scratch(ny, mats, rows, width):
     return [
-        pltpu.VMEM((g, mats, rows, width), BF16),
-        pltpu.VMEM((g, mats, rows, width), BF16),
+        pltpu.VMEM((ny, mats, rows, width), BF16),
+        pltpu.VMEM((ny, mats, rows, width), BF16),
+        pltpu.VMEM((2, mats, rows, width), BF16),
         pltpu.VMEM((mats, rows, width), BF16),
-        pltpu.VMEM((g, mats, rows, width), BF16),
+        pltpu.VMEM((ny, mats, rows, width), BF16),
     ]
 
 
@@ -215,7 +241,7 @@
     groups = lax.axis_size("dp")
     block = jax.ShapeDtypeStruct((peers, 2 * cols, t), BF16)
     links = pltpu.SemaphoreType.DMA((3,))
-    sums = pltpu.SemaphoreType.DMA((4,))
+    sums = pltpu.SemaphoreType.DMA((6,))
     (x,) = kernel_call(
         functools.partial(first_kernel, peers), [sent.reshape(block.shape)], [block], [links], 0
     )
@@ -234,8 +260,10 @@
     back = mm(
         "rc,ct->rt", jnp.concatenate([w_z, w_du], axis=1), jnp.concatenate([act, dpre], axis=0)
     )
-    r, mids = kernel_call(
-        functools.partial(middle_kernel, peers, groups),
+    width = tokens.shape[1]
+    ny = groups // 2
+    output, tok_grad, mids, ends = kernel_call(
+        functools.partial(rest_kernel, peers, groups),
         [
             back.reshape(block.shape),
             x,
@@ -243,24 +271,27 @@
             dpre.reshape(cols, hidden, t),
             q0,
             q1,
+            tokens,
+            out_grad,
+            p0,
+            p1,
+            w_out,
         ],
-        [block, jax.ShapeDtypeStruct((2 * cols, peers, hidden), F32)],
-        sum_scratch(groups, 2 * cols, peers // groups, hidden) + [links, sums],
+        [
+            jax.ShapeDtypeStruct((t, width), BF16),
+            jax.ShapeDtypeStruct((t, width), BF16),
+            jax.ShapeDtypeStruct((2 * cols, peers, hidden), F32),
+            jax.ShapeDtypeStruct((2, width, width), F32),
+        ],
+        [pltpu.VMEM(block.shape, BF16)]
+        + sum_scratch(ny, 2 * cols, peers // ny, hidden)
+        + sum_scratch(ny, 2, width // ny, width)
+        + [links, sums, sums],
         1,
     )
-    r = r.reshape(sent.shape)
-    width = tokens.shape[1]
-    (ends,) = kernel_call(
-        functools.partial(last_kernel, groups),
-        [r, tokens, out_grad, p0, p1],
-        [jax.ShapeDtypeStruct((2, width, width), F32)],
-        sum_scratch(groups, 2, width // groups, width) + [sums],
-        2,
-    )
-    outs = mm("rt,rc->tc", r, w_out)
     return (
-        outs[:, :width],
-        outs[:, width:],
+        output,
+        tok_grad,
         ends[1:],
         mids[:cols],
         mids[cols:].swapaxes(1, 2),

time: 135 us -> 120 us (0.89)
  Pallas kernels: 116 us -> 99.3 us
  local copies, waits for them, and re-layouts: 7.44 us -> 8.83 us
    pallas_call x3 -> x2, Pallas kernels: 116 us -> 99.3 us  [kernel_call(): pl.pallas_call(body, out_shape=outs, in_specs=[vmem] * len(ins), out_spec...]
    unnamed x18, local copies, waits for them, and re-layouts: 0.05 us -> 2.41 us
    dot_general x13 -> x12, matrix products: 8.16 us -> 7.8 us  [mm(): return jnp.einsum(spec, a, b, preferred_element_type=F32).astype(dtype)]
where the time goes in v3:
time: 120 us; the launch traced here: 119 us
  Pallas kernels  99.3 us (83%)
  local copies, waits for them, and re-layouts  8.83 us (7%)
  matrix products  7.8 us (6%)
  other arithmetic  2.27 us (2%)
    pallas_call x2, Pallas kernels, kernel_call(): pl.pallas_call(body, out_shape=outs, in_specs=[vmem] * len(ins), out_spec...  99.3 us
    dot_general x12, matrix products, mm(): return jnp.einsum(spec, a, b, preferred_element_type=F32).astype(dtype)  7.8 us
    unnamed x18, local copies, waits for them, and re-layouts  2.41 us

profile of v3, /device:TPU:64, one launch (start us, length us, event | category | flops | bytes accessed | tf_op | source)
XLA Modules:
  0.0 119.1 jit_solution(2672362974460005913)
XLA Ops:
  0.6 0.0 copy-start
  0.7 1.1 convolution_convert_fusion.7
  1.8 1.1 convolution_convert_fusion.9
  2.9 1.4 %convolution_convert_fusion.1 = bf16[256,1024]{1,0:T(8,128)(2,1)S(1)} fusion(bf16[1024,128]{1,0:T(8,128)(2,1)} %og.1, bf16[1024,128]{1,0:T(8,128)(2,1)} %tok.1, bf16[256,128]{1,0:T(8,128)(2,1)S(1)} %convolution_convert_fusion.9, bf16[256,128]{1,0:T(8,128)(2,1)S(1)} %convolution_convert_fusion.7), kind=kOutput, calls=%fused_computation.19 | convolution fusion | flops 135790592 | bytes 1179648 | tf_op jit(solution)/shard_map/rc,tc->rt/dot_general | solution.py:16
  4.3 1.0 reshape.42.src
  5.3 0.0 copy-start.4
  5.3 35.4 %shard_map.109 = bf16[64,4,1024]{2,1,0:T(4,128)(2,1)} custom-call(bf16[64,4,1024]{2,1,0:T(4,128)(2,1)} %reshape.42.src), custom_call_target="tpu_custom_call" | custom-call | tf_op jit(solution)/shard_map/pallas_call | solution.py:221
  40.7 1.2 reshape.43.x
  41.9 0.0 copy-start.1
  41.9 0.0 copy-done.4
  41.9 0.3 convolution_convert_fusion.3
  42.2 0.6 fusion.3
  42.8 0.0 copy-start.2
  42.8 0.0 copy-done
  42.8 0.3 convolution_convert_fusion.2
  43.1 0.0 copy-done.1
  43.1 1.0 fusion.8
  44.2 0.0 copy-start.3
  44.2 0.3 convolution_convert_fusion.5
  44.5 0.3 convolution_convert_fusion.4
  44.8 0.0 copy-done.2
  44.8 0.7 fusion.13
  45.5 0.0 copy-done.3
  45.5 0.0 copy-start.6
  45.5 0.0 copy-start.7
  45.5 1.0 reshape.45.src
  46.6 0.0 copy-done.6
  46.6 0.3 convolution_convert_fusion.6
  46.9 0.0 copy-done.7
  46.9 0.4 convolution_convert_fusion.8
  47.3 0.7 pad_maximum_fusion.w_out
  47.9 0.8 fusion.42
  48.8 0.7 fusion.27
  49.5 63.9 %shard_map.110 = (bf16[1024,128]{1,0:T(8,128)(2,1)}, bf16[1024,128]{1,0:T(8,128)(2,1)}, f32[4,64,256]{2,1,0:T(8,128)}, f32[2,128,128]{2,1,0:T(8,128)}) custom-call(bf16[64,4,1024]{2,1,0:T(4,128)(2,1)} %reshape.45.src, bf16[256,1024]{1,0:T(8,128)(2,1)} %copy-done.1, bf16[2,256,1024]{2,1,0:T(8,128)(2,1)} %bitcast.34, bf16[2,256,1024]{2,1,0:T(8,128)(2,1)} %bitcast.35, ...), custom_call_target="tpu_custom_call" | custom-call | tf_op jit(solution)/shard_map/pallas_call | solution.py:221
  113.4 0.0 copy-start.5
  113.4 1.7 %slice_bitcast_fusion = (f32[2,256,64]{1,2,0:T(8,128)}, f32[2,64,256]{2,1,0:T(8,128)}) fusion(f32[4,64,256]{2,1,0:T(8,128)} %get-tuple-element.13), kind=kLoop, calls=%fused_computation.43 | loop fusion | bytes 524288 | tf_op jit(solution)/shard_map/transpose | solution.py:297
  115.2 1.5 %fusion.47 = (f32[1,128,128]{2,1,0:T(8,128)}, f32[1,128,128]{2,1,0:T(8,128)}) fusion(f32[2,128,128]{2,1,0:T(8,128)} %get-tuple-element.12), kind=kLoop, calls=%fused_computation.72 | loop fusion | bytes 262144 | tf_op jit(solution)/shard_map/slice | solution.py:298
  116.7 1.7 %copy.18 = bf16[1024,128]{1,0:T(8,128)(2,1)} copy(bf16[1024,128]{1,0:T(8,128)(2,1)} %get-tuple-element.36) | data formatting | bytes 524288
  118.4 0.0 copy-done.5
  118.4 0.7 copy.19
  (5 shorter events, 0.0 us)
Async XLA Ops:
  0.6 42.2 %copy-start = (bf16[2,256,64]{1,2,0:T(8,128)(2,1)S(1)}, bf16[2,256,64]{1,2,0:T(8,128)(2,1)}, u32[]{:S(2)}) copy-start(bf16[2,256,64]{1,2,0:T(8,128)(2,1)} %param.9) | copy-start | bytes 196612
  5.3 36.6 %copy-start.4 = (bf16[2,64,256]{2,1,0:T(8,128)(2,1)S(1)}, bf16[2,64,256]{2,1,0:T(8,128)(2,1)}, u32[]{:S(2)}) copy-start(bf16[2,64,256]{2,1,0:T(8,128)(2,1)} %param.8) | copy-start | bytes 196612
  41.9 1.3 %copy-start.1 = (bf16[256,1024]{1,0:T(8,128)(2,1)}, bf16[256,1024]{1,0:T(8,128)(2,1)S(1)}, u32[]{:S(2)}) copy-start(bf16[256,1024]{1,0:T(8,128)(2,1)S(1)} %reshape.43.x) | copy-start | bytes 1572868
  42.8 2.0 %copy-start.2 = (bf16[512,1024]{1,0:T(8,128)(2,1)}, bf16[512,1024]{1,0:T(8,128)(2,1)S(1)}, u32[]{:S(2)}) copy-start(bf16[512,1024]{1,0:T(8,128)(2,1)S(1)} %get-tuple-element.20) | copy-start | bytes 3145732
  44.2 1.4 %copy-start.3 = (bf16[512,1024]{1,0:T(8,128)(2,1)}, bf16[512,1024]{1,0:T(8,128)(2,1)S(1)}, u32[]{:S(2)}) copy-start(bf16[512,1024]{1,0:T(8,128)(2,1)S(1)} %fusion.8) | copy-start | bytes 3145732
  45.5 1.0 copy-start.6
  45.5 1.4 %copy-start.7 = (bf16[1,128,128]{2,1,0:T(8,128)(2,1)S(1)}, bf16[1,128,128]{2,1,0:T(8,128)(2,1)}, u32[]{:S(2)}) copy-start(bf16[1,128,128]{2,1,0:T(8,128)(2,1)} %param.10) | copy-start | bytes 98308
  113.4 4.9 %copy-start.5 = (bf16[1024,128]{1,0:T(8,128)(2,1)S(1)}, bf16[1024,128]{1,0:T(8,128)(2,1)}, u32[]{:S(2)}) copy-start(bf16[1024,128]{1,0:T(8,128)(2,1)} %get-tuple-element.37) | copy-start | bytes 786436

commit v4 on v3

--- a/solution.py
+++ b/solution.py
@@ -3,6 +3,7 @@
 
 import jax
 import jax.numpy as jnp
+import numpy as np
 from jax import lax
 from jax.experimental import pallas as pl
 from jax.experimental.pallas import tpu as pltpu
@@ -12,30 +13,16 @@
 BF16 = jnp.bfloat16
 
 
-def mm(spec, a, b, dtype=BF16):
-    return jnp.einsum(spec, a, b, preferred_element_type=F32).astype(dtype)
-
-
 def cdf_part(value):
     return 0.5 * (1.0 + jax.scipy.special.erf(value / math.sqrt(2.0)))
 
 
-def gelu_deriv(value):
-    return cdf_part(value) + value * jnp.exp(-0.5 * value * value) / math.sqrt(2.0 * math.pi)
-
-
-def row_picks(peers, cols):
+def row_orders(peers, cols):
     rows = peers * 2 * cols
-    row = lax.broadcasted_iota(jnp.int32, (peers * cols, rows), 1)
-    unit = lax.broadcasted_iota(jnp.int32, (peers * cols, rows), 0)
-    flat = []
-    for which in range(2):
-        flat.append((row == (unit // cols) * (2 * cols) + which * cols + unit % cols).astype(BF16))
-    row = lax.broadcasted_iota(jnp.int32, (cols, peers, rows), 2)
-    peer = lax.broadcasted_iota(jnp.int32, (cols, peers, rows), 1)
-    col = lax.broadcasted_iota(jnp.int32, (cols, peers, rows), 0)
-    grouped = [(row == peer * (2 * cols) + which * cols + col).astype(BF16) for which in range(2)]
-    return flat, grouped
+    row = np.arange(rows).reshape(peers, 2, cols)
+    by_peer = np.eye(rows)[row.transpose(1, 0, 2).reshape(-1)]
+    by_col = np.eye(rows)[row.transpose(1, 2, 0).reshape(-1)]
+    return [jnp.asarray(m, BF16) for m in (by_peer.T, by_col, by_col.T, by_peer)]
 
 
 def greet(axis_sizes):
@@ -159,49 +146,72 @@
     return lax.dot_general(a, b, (((0,), (0,)), ((), ())), preferred_element_type=F32)
 
 
-def first_kernel(n, src, dst, sems):
-    greet((("tensor", n),))
-    greeted((("tensor", n),))
-    start_exchange(src, dst, sems, n, ((0, n // 2), (n // 2 + 1, n)))
-    keep_own(src, dst, sems).start()
-    end_exchange(src, dst, sems, n)
-
-
-def rest_kernel(
-    n, g, src, x, act, dpre, q0, q1, tok, og, p0, p1, w_out,
-    output, tok_grad, mids, ends,
-    dst, flat, land, pair, total, gath, flat2, land2, pair2, total2, gath2, links, sums, sums2,
+def whole_kernel(
+    n, g, tok, og, fu, su, fdt, sd, pack_in, unpack_mid, pack_mid, unpack_end,
+    zdu, mids, ends,
+    src, dst, src2, dst2, cols_x, act, dpre,
+    flat, land, pair, total, gath, flat2, land2, pair2, total2, gath2,
+    links, links2, sums, sums2,
 ):
     axes = (("tensor", n), ("dp", g))
     ny = g // 2
-    cols = q0.shape[0]
-    rows, hidden = flat.shape[2:]
-    width = tok.shape[1]
+    cols, _, hidden = su.shape
+    t, width = tok.shape
+    rows = flat.shape[2]
+    step = 256
     greet(axes)
+    for c in range(0, t, step):
+        span = pl.ds(c, step)
+        u = lax.dot_general(fu[0], tok[span], (((0,), (1,)), ((), ())), preferred_element_type=F32)
+        dz = dot_nt(sd[0], og[span])
+        both = jnp.concatenate([u, dz], axis=0).astype(BF16)
+        src[:, :, span] = dot(pack_in[...], both).astype(BF16).reshape(n, 2 * cols, step)
+    greeted(axes)
+    start_exchange(src, dst, links, n, ((0, n // 2), (n // 2 + 1, n)))
+    keep_own(src, dst, links).start()
+    end_exchange(src, dst, links, n)
+
+    for c in range(0, t, step):
+        span = pl.ds(c, step)
+        x = dst[:, :, span].reshape(n * 2 * cols, step)
+        x = dot(unpack_mid[...], x).astype(BF16)
+        cols_x[:, span] = x
+        zs, dus = [], []
+        for j in range(cols):
+            u = x[j * n : (j + 1) * n]
+            dz = x[(cols + j) * n : (cols + j + 1) * n]
+            pre = dot_tn(su[j], u).astype(BF16).astype(F32)
+            phi = cdf_part(pre)
+            a = (pre * phi).astype(BF16)
+            slope = phi + pre * jnp.exp(-0.5 * pre * pre) / math.sqrt(2.0 * math.pi)
+            d = (dot_tn(fdt[j], dz) * slope).astype(BF16)
+            act[j, :, span] = a
+            dpre[j, :, span] = d
+            zs.append(dot(fdt[j], a))
+            dus.append(dot(su[j], d))
+        back = jnp.concatenate(zs + dus, axis=0).astype(BF16)
+        src2[:, :, span] = dot(pack_mid[...], back).astype(BF16).reshape(n, 2 * cols, step)
+    start_exchange(src2, dst2, links2, n, ((0, n // 4), (n // 2 + 1, n)))
+    keep_own(src2, dst2, links2).start()
+
     for j in range(cols):
-        u = dot(q0[j], x[...]).astype(BF16)
-        dz = dot(q1[j], x[...]).astype(BF16)
+        u = cols_x[j * n : (j + 1) * n]
+        dz = cols_x[(cols + j) * n : (cols + j + 1) * n]
         flat[:, j] = dot_nt(u, dpre[j]).reshape(ny, rows, hidden).astype(BF16)
         flat[:, cols + j] = dot_nt(dz, act[j]).reshape(ny, rows, hidden).astype(BF16)
-    greeted(axes)
     sum_scatter(flat, land, sums, ny)
-    start_exchange(src, dst, links, n, ((0, n // 4), (n // 2 + 1, n)))
-    keep_own(src, dst, links).start()
     sum_swap(flat, land, pair, sums, ny)
-    start_exchange(src, dst, links, n, ((n // 4, n // 2),))
+    start_exchange(src2, dst2, links2, n, ((n // 4, n // 2),))
     sum_spread(pair, total, gath, sums, ny)
     sum_end(gath, mids, sums, ny)
-    end_exchange(src, dst, links, n)
-
-    r = dst[...].reshape(n * dst.shape[1], dst.shape[2])
-    z = dot(p0[...], r).astype(BF16)
-    flat2[:, 0] = dot(z, og[...]).reshape(ny, width // ny, width).astype(BF16)
-    du = dot(p1[...], r).astype(BF16)
-    flat2[:, 1] = dot(du, tok[...]).T.reshape(ny, width // ny, width).astype(BF16)
+    end_exchange(src2, dst2, links2, n)
+
+    r = dot(unpack_end[...], dst2[...].reshape(n * 2 * cols, t)).astype(BF16)
+    flat2[:, 0] = dot(r[:width], og[...]).reshape(ny, width // ny, width).astype(BF16)
+    flat2[:, 1] = dot(r[width:], tok[...]).T.reshape(ny, width // ny, width).astype(BF16)
     sum_scatter(flat2, land2, sums2, ny)
-    output[...] = dot_tn(r, w_out[:, :width]).astype(BF16)
+    zdu[...] = r
     sum_swap(flat2, land2, pair2, sums2, ny)
-    tok_grad[...] = dot_tn(r, w_out[:, width:]).astype(BF16)
     sum_spread(pair2, total2, gath2, sums2, ny)
     sum_end(gath2, ends, sums2, ny)
 
@@ -230,68 +240,42 @@
 
 def shards(tokens, first_up, second_up, first_down, second_down, out_grad):
     peers = lax.axis_size("tensor")
-    t = tokens.shape[0]
+    groups = lax.axis_size("dp")
+    t, width = tokens.shape
     cols, _, hidden = second_up.shape
-    fu, sd = first_up[0], second_down[0]
-    (p0, p1), (q0, q1) = row_picks(peers, cols)
-
-    both = jnp.concatenate([tokens, out_grad], axis=1)
-    w_in = jnp.concatenate([mm("jr,ij->ri", p0, fu), mm("jr,jk->rk", p1, sd)], axis=1)
-    sent = mm("rc,tc->rt", w_in, both)
-    groups = lax.axis_size("dp")
-    block = jax.ShapeDtypeStruct((peers, 2 * cols, t), BF16)
+    ny = groups // 2
+    rows = peers * 2 * cols
+    block = pltpu.VMEM((peers, 2 * cols, t), BF16)
     links = pltpu.SemaphoreType.DMA((3,))
     sums = pltpu.SemaphoreType.DMA((6,))
-    (x,) = kernel_call(
-        functools.partial(first_kernel, peers), [sent.reshape(block.shape)], [block], [links], 0
-    )
-    x = x.reshape(sent.shape)
-
-    w_pre = mm("jbr,jbo->jor", q0, second_up).reshape(cols * hidden, -1)
-    w_dact = mm("jbr,job->jor", q1, first_down).reshape(cols * hidden, -1)
-    w_z = mm("jbr,job->rjo", q0, first_down).reshape(-1, cols * hidden)
-    w_du = mm("jbr,jbo->rjo", q1, second_up).reshape(-1, cols * hidden)
-    w_out = jnp.concatenate([mm("jr,jk->rk", p0, sd), mm("jr,ij->ri", p1, fu)], axis=1)
-
-    pre = mm("or,rt->ot", w_pre, x).astype(F32)
-    act = (pre * cdf_part(pre)).astype(BF16)
-    dact = mm("or,rt->ot", w_dact, x, F32)
-    dpre = (dact * gelu_deriv(pre)).astype(BF16)
-    back = mm(
-        "rc,ct->rt", jnp.concatenate([w_z, w_du], axis=1), jnp.concatenate([act, dpre], axis=0)
-    )
-    width = tokens.shape[1]
-    ny = groups // 2
-    output, tok_grad, mids, ends = kernel_call(
-        functools.partial(rest_kernel, peers, groups),
+    zdu, mids, ends = kernel_call(
+        functools.partial(whole_kernel, peers, groups),
+        [tokens, out_grad, first_up, second_up, first_down.swapaxes(1, 2), second_down]
+        + row_orders(peers, cols),
         [
-            back.reshape(block.shape),
-            x,
-            act.reshape(cols, hidden, t),
-            dpre.reshape(cols, hidden, t),
-            q0,
-            q1,
-            tokens,
-            out_grad,
-            p0,
-            p1,
-            w_out,
-        ],
-        [
-            jax.ShapeDtypeStruct((t, width), BF16),
-            jax.ShapeDtypeStruct((t, width), BF16),
+            jax.ShapeDtypeStruct((rows, t), BF16),
             jax.ShapeDtypeStruct((2 * cols, peers, hidden), F32),
             jax.ShapeDtypeStruct((2, width, width), F32),
         ],
-        [pltpu.VMEM(block.shape, BF16)]
+        [
+            block,
+            block,
+            block,
+            block,
+            pltpu.VMEM((rows, t), BF16),
+            pltpu.VMEM((cols, hidden, t), BF16),
+            pltpu.VMEM((cols, hidden, t), BF16),
+        ]
         + sum_scratch(ny, 2 * cols, peers // ny, hidden)
         + sum_scratch(ny, 2, width // ny, width)
-        + [links, sums, sums],
-        1,
-    )
+        + [links, links, sums, sums],
+        0,
+    )
+    output = jnp.einsum("jt,jk->tk", zdu[:width], second_down[0], preferred_element_type=F32)
+    tok_grad = jnp.einsum("jt,ij->ti", zdu[width:], first_up[0], preferred_element_type=F32)
     return (
-        output,
-        tok_grad,
+        output.astype(BF16),
+        tok_grad.astype(BF16),
         ends[1:],
         mids[:cols],
         mids[cols:].swapaxes(1, 2),

time: 120 us -> 99.8 us (0.83)
  local copies, waits for them, and re-layouts: 8.83 us -> 2.32 us
  Pallas kernels: 99.3 us -> 93.7 us
  matrix products: 7.8 us -> 2.88 us
  other arithmetic: 2.27 us -> 0 us
    pallas_call x2 -> x1, Pallas kernels: 99.3 us -> 93.7 us  [kernel_call(): pl.pallas_call(body, out_shape=outs, in_specs=[vmem] * len(ins), out_spec...]
    dot_general x12 -> x2, matrix products: 7.8 us -> 2.88 us  [the longest x1 1.92 us: shards(): jnp.einsum('jt,ij->ti', zdu[width:], first_up[0], preferred_element_type=...]
    reshape x3 -> x0, local copies, waits for them, and re-layouts: 3.16 us -> none  [the longest x1 1.16 us: shards(): x = x.reshape(sent.shape)]
    unnamed x18 -> x8, local copies, waits for them, and re-layouts: 2.41 us -> 0.02 us
    convert_element_type x2 -> x0, other arithmetic: 1.57 us -> none  [the longest x1 0.82 us: row_picks(): (row == unit // cols * (2 * cols) + which * cols + unit % cols).astype(BF16)]
where the time goes in v4:
time: 99.8 us; the launch traced here: 99.5 us
  Pallas kernels  93.7 us (94%)
  matrix products  2.88 us (3%)
  local copies, waits for them, and re-layouts  2.32 us (2%)
    pallas_call x1, Pallas kernels, kernel_call(): pl.pallas_call(body, out_shape=outs, in_specs=[vmem] * len(ins), out_spec...  93.7 us

profile of v4, /device:TPU:64, one launch (start us, length us, event | category | flops | bytes accessed | tf_op | source)
XLA Modules:
  0.0 99.5 jit_solution(16147587621039972756)
XLA Ops:
  0.6 0.0 copy-start.2
  0.6 93.7 %shard_map.145 = (bf16[256,1024]{1,0:T(8,128)(2,1)}, f32[4,64,256]{2,1,0:T(8,128)}, f32[2,128,128]{2,1,0:T(8,128)}) custom-call(bf16[1024,128]{1,0:T(8,128)(2,1)} %tok.1, bf16[1024,128]{1,0:T(8,128)(2,1)} %og.1, bf16[1,128,128]{2,1,0:T(8,128)(2,1)} %fu.1, bf16[2,64,256]{2,1,0:T(8,128)(2,1)} %su.1, bf16[2,64,256]{2,1,0:T(8,128)(2,1)} %bitcast.9, ...), custom_call_target="tpu_custom_call" | custom-call | tf_op jit(solution)/shard_map/pallas_call | solution.py:231
  94.3 0.0 copy-start
  94.3 1.6 %fusion.4 = (f32[1,128,128]{2,1,0:T(8,128)}, f32[1,128,128]{2,1,0:T(8,128)}) fusion(f32[2,128,128]{2,1,0:T(8,128)} %get-tuple-element.10), kind=kLoop, calls=%fused_computation.7 | loop fusion | bytes 262144 | tf_op jit(solution)/shard_map/slice | solution.py:282
  95.9 0.0 copy-done.2
  95.9 0.0 copy-start.3
  95.9 1.9 %convolution_convert_fusion = bf16[1024,128]{1,0:T(8,128)(2,1)} fusion(bf16[256,1024]{1,0:T(8,128)(2,1)} %get-tuple-element.9, bf16[1,128,128]{2,1,0:T(8,128)(2,1)S(1)} %copy-done.2), kind=kOutput, calls=%fused_computation | convolution fusion | flops 33685504 | bytes 557056 | tf_op jit(solution)/shard_map/jt,ij->ti/dot_general | solution.py:275
  97.8 0.0 copy-done
  97.8 0.0 copy-done.3
  97.8 0.0 copy-start.1
  97.8 1.0 convolution_convert_fusion.1
  98.8 0.0 copy-done.1
  98.8 0.7 slice_bitcast_fusion
Async XLA Ops:
  0.6 95.3 %copy-start.2 = (bf16[1,128,128]{2,1,0:T(8,128)(2,1)S(1)}, bf16[1,128,128]{2,1,0:T(8,128)(2,1)}, u32[]{:S(2)}) copy-start(bf16[1,128,128]{2,1,0:T(8,128)(2,1)} %fu.1) | copy-start | bytes 98308
  94.3 3.5 %copy-start = (bf16[256,1024]{1,0:T(8,128)(2,1)S(1)}, bf16[256,1024]{1,0:T(8,128)(2,1)}, u32[]{:S(2)}) copy-start(bf16[256,1024]{1,0:T(8,128)(2,1)} %get-tuple-element.9) | copy-start | bytes 1572868
  95.9 1.9 %copy-start.3 = (bf16[1,128,128]{2,1,0:T(8,128)(2,1)S(1)}, bf16[1,128,128]{2,1,0:T(8,128)(2,1)}, u32[]{:S(2)}) copy-start(bf16[1,128,128]{2,1,0:T(8,128)(2,1)} %sd.1) | copy-start | bytes 98308
  97.8 1.0 copy-start.1

commit v5 on v4

--- a/solution.py
+++ b/solution.py
@@ -151,29 +151,22 @@
     zdu, mids, ends,
     src, dst, src2, dst2, cols_x, act, dpre,
     flat, land, pair, total, gath, flat2, land2, pair2, total2, gath2,
-    links, links2, sums, sums2,
+    sums, sums2, *links,
 ):
     axes = (("tensor", n), ("dp", g))
     ny = g // 2
     cols, _, hidden = su.shape
     t, width = tok.shape
     rows = flat.shape[2]
+    parts = src.shape[0]
+    part = t // parts
     step = 256
-    greet(axes)
-    for c in range(0, t, step):
-        span = pl.ds(c, step)
-        u = lax.dot_general(fu[0], tok[span], (((0,), (1,)), ((), ())), preferred_element_type=F32)
-        dz = dot_nt(sd[0], og[span])
-        both = jnp.concatenate([u, dz], axis=0).astype(BF16)
-        src[:, :, span] = dot(pack_in[...], both).astype(BF16).reshape(n, 2 * cols, step)
-    greeted(axes)
-    start_exchange(src, dst, links, n, ((0, n // 2), (n // 2 + 1, n)))
-    keep_own(src, dst, links).start()
-    end_exchange(src, dst, links, n)
-
-    for c in range(0, t, step):
-        span = pl.ds(c, step)
-        x = dst[:, :, span].reshape(n * 2 * cols, step)
+    there, back_again = links[:parts], links[parts:]
+
+    def middle(h, c):
+        inner = pl.ds(c, step)
+        span = pl.ds(h * part + c, step)
+        x = dst[h, :, :, inner].reshape(n * 2 * cols, step)
         x = dot(unpack_mid[...], x).astype(BF16)
         cols_x[:, span] = x
         zs, dus = [], []
@@ -190,9 +183,28 @@
             zs.append(dot(fdt[j], a))
             dus.append(dot(su[j], d))
         back = jnp.concatenate(zs + dus, axis=0).astype(BF16)
-        src2[:, :, span] = dot(pack_mid[...], back).astype(BF16).reshape(n, 2 * cols, step)
-    start_exchange(src2, dst2, links2, n, ((0, n // 4), (n // 2 + 1, n)))
-    keep_own(src2, dst2, links2).start()
+        src2[h, :, :, inner] = dot(pack_mid[...], back).astype(BF16).reshape(n, 2 * cols, step)
+
+    greet(axes)
+    for c in range(0, t, step):
+        span = pl.ds(c, step)
+        u = lax.dot_general(fu[0], tok[span], (((0,), (1,)), ((), ())), preferred_element_type=F32)
+        dz = dot_nt(sd[0], og[span])
+        both = jnp.concatenate([u, dz], axis=0).astype(BF16)
+        both = dot(pack_in[...], both).astype(BF16).reshape(n, 2 * cols, step)
+        src[c // part, :, :, pl.ds(c % part, step)] = both
+    greeted(axes)
+    for h in range(parts):
+        start_exchange(src.at[h], dst.at[h], there[h], n, ((0, n // 2), (n // 2 + 1, n)))
+        keep_own(src.at[h], dst.at[h], there[h]).start()
+    for h in range(parts):
+        end_exchange(src.at[h], dst.at[h], there[h], n)
+        for c in range(0, part, step):
+            middle(h, c)
+        last = h == parts - 1
+        spans = ((0, n // 4 if last else n // 2), (n // 2 + 1, n))
+        start_exchange(src2.at[h], dst2.at[h], back_again[h], n, spans)
+        keep_own(src2.at[h], dst2.at[h], back_again[h]).start()
 
     for j in range(cols):
         u = cols_x[j * n : (j + 1) * n]
@@ -201,16 +213,24 @@
         flat[:, cols + j] = dot_nt(dz, act[j]).reshape(ny, rows, hidden).astype(BF16)
     sum_scatter(flat, land, sums, ny)
     sum_swap(flat, land, pair, sums, ny)
-    start_exchange(src2, dst2, links2, n, ((n // 4, n // 2),))
-    sum_spread(pair, total, gath, sums, ny)
-    sum_end(gath, mids, sums, ny)
-    end_exchange(src2, dst2, links2, n)
-
-    r = dot(unpack_end[...], dst2[...].reshape(n * 2 * cols, t)).astype(BF16)
-    flat2[:, 0] = dot(r[:width], og[...]).reshape(ny, width // ny, width).astype(BF16)
-    flat2[:, 1] = dot(r[width:], tok[...]).T.reshape(ny, width // ny, width).astype(BF16)
+    h = parts - 1
+    start_exchange(src2.at[h], dst2.at[h], back_again[h], n, ((n // 4, n // 2),))
+
+    down = jnp.zeros((width, width), F32)
+    up = jnp.zeros((width, width), F32)
+    for h in range(parts):
+        if h == parts - 1:
+            sum_spread(pair, total, gath, sums, ny)
+            sum_end(gath, mids, sums, ny)
+        end_exchange(src2.at[h], dst2.at[h], back_again[h], n)
+        span = pl.ds(h * part, part)
+        r = dot(unpack_end[...], dst2[h].reshape(n * 2 * cols, part)).astype(BF16)
+        zdu[:, span] = r
+        down = down + dot(r[:width], og[span])
+        up = up + dot(r[width:], tok[span])
+    flat2[:, 0] = down.reshape(ny, width // ny, width).astype(BF16)
+    flat2[:, 1] = up.T.reshape(ny, width // ny, width).astype(BF16)
     sum_scatter(flat2, land2, sums2, ny)
-    zdu[...] = r
     sum_swap(flat2, land2, pair2, sums2, ny)
     sum_spread(pair2, total2, gath2, sums2, ny)
     sum_end(gath2, ends, sums2, ny)
@@ -245,7 +265,8 @@
     cols, _, hidden = second_up.shape
     ny = groups // 2
     rows = peers * 2 * cols
-    block = pltpu.VMEM((peers, 2 * cols, t), BF16)
+    parts = 2
+    block = pltpu.VMEM((parts, peers, 2 * cols, t // parts), BF16)
     links = pltpu.SemaphoreType.DMA((3,))
     sums = pltpu.SemaphoreType.DMA((6,))
     zdu, mids, ends = kernel_call(
@@ -268,7 +289,8 @@
         ]
         + sum_scratch(ny, 2 * cols, peers // ny, hidden)
         + sum_scratch(ny, 2, width // ny, width)
-        + [links, links, sums, sums],
+        + [sums, sums]
+        + [links] * (2 * parts),
         0,
     )
     output = jnp.einsum("jt,jk->tk", zdu[:width], second_down[0], preferred_element_type=F32)

time: 99.8 us -> 93.9 us (0.941)
  the two profiles are of different devices: /device:TPU:64 before, /device:TPU:68 now
where the time goes in v5:
time: 93.9 us; the launch traced here: 93.6 us
  Pallas kernels  87.8 us (94%)
  matrix products  2.88 us (3%)
  local copies, waits for them, and re-layouts  2.32 us (2%)
    pallas_call x1, Pallas kernels, kernel_call(): pl.pallas_call(body, out_shape=outs, in_specs=[vmem] * len(ins), out_spec...  87.8 us
    dot_general x1, matrix products, shards(): jnp.einsum('jt,ij->ti', zdu[width:], first_up[0], preferred_element_type=...  1.92 us

profile of v5, /device:TPU:68, one launch (start us, length us, event | category | flops | bytes accessed | tf_op | source)
XLA Modules:
  0.0 93.6 jit_solution(1656645852152654417)
XLA Ops:
  0.6 0.0 copy-start.2
  0.6 87.8 %shard_map.145 = (bf16[256,1024]{1,0:T(8,128)(2,1)}, f32[4,64,256]{2,1,0:T(8,128)}, f32[2,128,128]{2,1,0:T(8,128)}) custom-call(bf16[1024,128]{1,0:T(8,128)(2,1)} %tok.1, bf16[1024,128]{1,0:T(8,128)(2,1)} %og.1, bf16[1,128,128]{2,1,0:T(8,128)(2,1)} %fu.1, bf16[2,64,256]{2,1,0:T(8,128)(2,1)} %su.1, bf16[2,64,256]{2,1,0:T(8,128)(2,1)} %bitcast.9, ...), custom_call_target="tpu_custom_call" | custom-call | tf_op jit(solution)/shard_map/pallas_call | solution.py:251
  88.4 0.0 copy-start
  88.4 1.6 %fusion.4 = (f32[1,128,128]{2,1,0:T(8,128)}, f32[1,128,128]{2,1,0:T(8,128)}) fusion(f32[2,128,128]{2,1,0:T(8,128)} %get-tuple-element.10), kind=kLoop, calls=%fused_computation.7 | loop fusion | bytes 262144 | tf_op jit(solution)/shard_map/slice | solution.py:304
  90.0 0.0 copy-done.2
  90.0 0.0 copy-start.3
  90.0 1.9 %convolution_convert_fusion = bf16[1024,128]{1,0:T(8,128)(2,1)} fusion(bf16[256,1024]{1,0:T(8,128)(2,1)} %get-tuple-element.9, bf16[1,128,128]{2,1,0:T(8,128)(2,1)S(1)} %copy-done.2), kind=kOutput, calls=%fused_computation | convolution fusion | flops 33685504 | bytes 557056 | tf_op jit(solution)/shard_map/jt,ij->ti/dot_general | solution.py:297
  91.9 0.0 copy-done
  91.9 0.0 copy-done.3
  91.9 0.0 copy-start.1
  91.9 1.0 %convolution_convert_fusion.1 = bf16[1024,128]{1,0:T(8,128)(2,1)} fusion(bf16[256,1024]{1,0:T(8,128)(2,1)S(1)} %copy-done, bf16[1,128,128]{2,1,0:T(8,128)(2,1)S(1)} %copy-done.3), kind=kOutput, calls=%fused_computation.1 | convolution fusion | flops 33685504 | bytes 557056 | tf_op jit(solution)/shard_map/jt,jk->tk/dot_general | solution.py:296
  92.9 0.0 copy-done.1
  92.9 0.7 slice_bitcast_fusion
Async XLA Ops:
  0.6 89.4 %copy-start.2 = (bf16[1,128,128]{2,1,0:T(8,128)(2,1)S(1)}, bf16[1,128,128]{2,1,0:T(8,128)(2,1)}, u32[]{:S(2)}) copy-start(bf16[1,128,128]{2,1,0:T(8,128)(2,1)} %fu.1) | copy-start | bytes 98308
  88.4 3.5 %copy-start = (bf16[256,1024]{1,0:T(8,128)(2,1)S(1)}, bf16[256,1024]{1,0:T(8,128)(2,1)}, u32[]{:S(2)}) copy-start(bf16[256,1024]{1,0:T(8,128)(2,1)} %get-tuple-element.9) | copy-start | bytes 1572868
  90.0 1.9 %copy-start.3 = (bf16[1,128,128]{2,1,0:T(8,128)(2,1)S(1)}, bf16[1,128,128]{2,1,0:T(8,128)(2,1)}, u32[]{:S(2)}) copy-start(bf16[1,128,128]{2,1,0:T(8,128)(2,1)} %sd.1) | copy-start | bytes 98308
  91.9 1.0 %copy-start.1 = (f32[4,64,256]{2,1,0:T(8,128)S(1)}, f32[4,64,256]{2,1,0:T(8,128)}, u32[]{:S(2)}) copy-start(f32[4,64,256]{2,1,0:T(8,128)} %get-tuple-element.11) | copy-start | bytes 786436

commit v6 on v5

--- a/solution.py
+++ b/solution.py
@@ -32,11 +32,12 @@
 
         def tell(k, carry, axis=axis, n=n, me=me):
             pl.semaphore_signal(
-                barrier, inc=1, device_id={axis: (me + k) % n}, device_id_type=pl.DeviceIdType.MESH
+                barrier, inc=1, device_id={axis: (me + n // 2 + k) % n}, device_id_type=pl.DeviceIdType.MESH
             )
             return carry
 
-        lax.fori_loop(1, n, tell, 0)
+        lax.fori_loop(0, n // 2, tell, 0)
+        lax.fori_loop(n // 2 + 1, n, tell, 0)
 
 
 def greeted(axis_sizes):
@@ -153,7 +154,7 @@
     flat, land, pair, total, gath, flat2, land2, pair2, total2, gath2,
     sums, sums2, *links,
 ):
-    axes = (("tensor", n), ("dp", g))
+    axes = (("dp", g), ("tensor", n))
     ny = g // 2
     cols, _, hidden = su.shape
     t, width = tok.shape
@@ -265,7 +266,7 @@
     cols, _, hidden = second_up.shape
     ny = groups // 2
     rows = peers * 2 * cols
-    parts = 2
+    parts = 4
     block = pltpu.VMEM((parts, peers, 2 * cols, t // parts), BF16)
     links = pltpu.SemaphoreType.DMA((3,))
     sums = pltpu.SemaphoreType.DMA((6,))

time: 93.9 us -> 94.5 us (level)
  the two profiles are of different devices: /device:TPU:68 before, /device:TPU:6 now
where the time goes in v6:
time: 94.5 us; the launch traced here: 94.3 us
  Pallas kernels  88.4 us (94%)
  matrix products  2.88 us (3%)
  local copies, waits for them, and re-layouts  2.32 us (2%)
    pallas_call x1, Pallas kernels, kernel_call(): pl.pallas_call(body, out_shape=outs, in_specs=[vmem] * len(ins), out_spec...  88.4 us
    dot_general x1, matrix products, shards(): jnp.einsum('jt,ij->ti', zdu[width:], first_up[0], preferred_element_type=...  1.92 us

profile of v6, /device:TPU:6, one launch (start us, length us, event | category | flops | bytes accessed | tf_op | source)
XLA Modules:
  0.0 94.3 jit_solution(11443684251135005745)
XLA Ops:
  0.6 0.0 copy-start.2
  0.6 88.4 %shard_map.145 = (bf16[256,1024]{1,0:T(8,128)(2,1)}, f32[4,64,256]{2,1,0:T(8,128)}, f32[2,128,128]{2,1,0:T(8,128)}) custom-call(bf16[1024,128]{1,0:T(8,128)(2,1)} %tok.1, bf16[1024,128]{1,0:T(8,128)(2,1)} %og.1, bf16[1,128,128]{2,1,0:T(8,128)(2,1)} %fu.1, bf16[2,64,256]{2,1,0:T(8,128)(2,1)} %su.1, bf16[2,64,256]{2,1,0:T(8,128)(2,1)} %bitcast.9, ...), custom_call_target="tpu_custom_call" | custom-call | tf_op jit(solution)/shard_map/pallas_call | solution.py:252
  89.1 0.0 copy-start
  89.1 1.6 %fusion.4 = (f32[1,128,128]{2,1,0:T(8,128)}, f32[1,128,128]{2,1,0:T(8,128)}) fusion(f32[2,128,128]{2,1,0:T(8,128)} %get-tuple-element.10), kind=kLoop, calls=%fused_computation.7 | loop fusion | bytes 262144 | tf_op jit(solution)/shard_map/slice | solution.py:305
  90.7 0.0 copy-done.2
  90.7 0.0 copy-start.3
  90.7 1.9 %convolution_convert_fusion = bf16[1024,128]{1,0:T(8,128)(2,1)} fusion(bf16[256,1024]{1,0:T(8,128)(2,1)} %get-tuple-element.9, bf16[1,128,128]{2,1,0:T(8,128)(2,1)S(1)} %copy-done.2), kind=kOutput, calls=%fused_computation | convolution fusion | flops 33685504 | bytes 557056 | tf_op jit(solution)/shard_map/jt,ij->ti/dot_general | solution.py:298
  92.6 0.0 copy-done
  92.6 0.0 copy-done.3
  92.6 0.0 copy-start.1
  92.6 1.0 %convolution_convert_fusion.1 = bf16[1024,128]{1,0:T(8,128)(2,1)} fusion(bf16[256,1024]{1,0:T(8,128)(2,1)S(1)} %copy-done, bf16[1,128,128]{2,1,0:T(8,128)(2,1)S(1)} %copy-done.3), kind=kOutput, calls=%fused_computation.1 | convolution fusion | flops 33685504 | bytes 557056 | tf_op jit(solution)/shard_map/jt,jk->tk/dot_general | solution.py:297
  93.6 0.0 copy-done.1
  93.6 0.7 slice_bitcast_fusion
Async XLA Ops:
  0.6 90.1 %copy-start.2 = (bf16[1,128,128]{2,1,0:T(8,128)(2,1)S(1)}, bf16[1,128,128]{2,1,0:T(8,128)(2,1)}, u32[]{:S(2)}) copy-start(bf16[1,128,128]{2,1,0:T(8,128)(2,1)} %fu.1) | copy-start | bytes 98308
  89.1 3.5 %copy-start = (bf16[256,1024]{1,0:T(8,128)(2,1)S(1)}, bf16[256,1024]{1,0:T(8,128)(2,1)}, u32[]{:S(2)}) copy-start(bf16[256,1024]{1,0:T(8,128)(2,1)} %get-tuple-element.9) | copy-start | bytes 1572868
  90.7 1.9 %copy-start.3 = (bf16[1,128,128]{2,1,0:T(8,128)(2,1)S(1)}, bf16[1,128,128]{2,1,0:T(8,128)(2,1)}, u32[]{:S(2)}) copy-start(bf16[1,128,128]{2,1,0:T(8,128)(2,1)} %sd.1) | copy-start | bytes 98308
  92.6 1.0 %copy-start.1 = (f32[4,64,256]{2,1,0:T(8,128)S(1)}, f32[4,64,256]{2,1,0:T(8,128)}, u32[]{:S(2)}) copy-start(f32[4,64,256]{2,1,0:T(8,128)} %get-tuple-element.11) | copy-start | bytes 786436

commit v7 on v6

--- a/solution.py
+++ b/solution.py
@@ -203,7 +203,7 @@
         for c in range(0, part, step):
             middle(h, c)
         last = h == parts - 1
-        spans = ((0, n // 4 if last else n // 2), (n // 2 + 1, n))
+        spans = ((0, 3 * n // 8 if last else n // 2), (n // 2 + 1, n))
         start_exchange(src2.at[h], dst2.at[h], back_again[h], n, spans)
         keep_own(src2.at[h], dst2.at[h], back_again[h]).start()
 
@@ -215,7 +215,7 @@
     sum_scatter(flat, land, sums, ny)
     sum_swap(flat, land, pair, sums, ny)
     h = parts - 1
-    start_exchange(src2.at[h], dst2.at[h], back_again[h], n, ((n // 4, n // 2),))
+    start_exchange(src2.at[h], dst2.at[h], back_again[h], n, ((3 * n // 8, n // 2),))
 
     down = jnp.zeros((width, width), F32)
     up = jnp.zeros((width, width), F32)
@@ -266,7 +266,7 @@
     cols, _, hidden = second_up.shape
     ny = groups // 2
     rows = peers * 2 * cols
-    parts = 4
+    parts = 2
     block = pltpu.VMEM((parts, peers, 2 * cols, t // parts), BF16)
     links = pltpu.SemaphoreType.DMA((3,))
     sums = pltpu.SemaphoreType.DMA((6,))

time: 94.5 us -> 92.5 us (0.979)
  the two profiles are of different devices: /device:TPU:6 before, /device:TPU:66 now
where the time goes in v7:
time: 92.5 us; the launch traced here: 92.3 us
  Pallas kernels  86.4 us (93%)
  matrix products  2.88 us (3%)
  local copies, waits for them, and re-layouts  2.32 us (3%)
    pallas_call x1, Pallas kernels, kernel_call(): pl.pallas_call(body, out_shape=outs, in_specs=[vmem] * len(ins), out_spec...  86.4 us
    dot_general x1, matrix products, shards(): jnp.einsum('jt,ij->ti', zdu[width:], first_up[0], preferred_element_type=...  1.92 us

profile of v7, /device:TPU:66, one launch (start us, length us, event | category | flops | bytes accessed | tf_op | source)
XLA Modules:
  0.0 92.3 jit_solution(7673804661178153944)
XLA Ops:
  0.6 0.0 copy-start.2
  0.6 86.4 %shard_map.145 = (bf16[256,1024]{1,0:T(8,128)(2,1)}, f32[4,64,256]{2,1,0:T(8,128)}, f32[2,128,128]{2,1,0:T(8,128)}) custom-call(bf16[1024,128]{1,0:T(8,128)(2,1)} %tok.1, bf16[1024,128]{1,0:T(8,128)(2,1)} %og.1, bf16[1,128,128]{2,1,0:T(8,128)(2,1)} %fu.1, bf16[2,64,256]{2,1,0:T(8,128)(2,1)} %su.1, bf16[2,64,256]{2,1,0:T(8,128)(2,1)} %bitcast.9, ...), custom_call_target="tpu_custom_call" | custom-call | tf_op jit(solution)/shard_map/pallas_call | solution.py:252
  87.1 0.0 copy-start
  87.1 1.6 %fusion.4 = (f32[1,128,128]{2,1,0:T(8,128)}, f32[1,128,128]{2,1,0:T(8,128)}) fusion(f32[2,128,128]{2,1,0:T(8,128)} %get-tuple-element.10), kind=kLoop, calls=%fused_computation.7 | loop fusion | bytes 262144 | tf_op jit(solution)/shard_map/slice | solution.py:305
  88.7 0.0 copy-done.2
  88.7 0.0 copy-start.3
  88.7 1.9 %convolution_convert_fusion = bf16[1024,128]{1,0:T(8,128)(2,1)} fusion(bf16[256,1024]{1,0:T(8,128)(2,1)} %get-tuple-element.9, bf16[1,128,128]{2,1,0:T(8,128)(2,1)S(1)} %copy-done.2), kind=kOutput, calls=%fused_computation | convolution fusion | flops 33685504 | bytes 557056 | tf_op jit(solution)/shard_map/jt,ij->ti/dot_general | solution.py:298
  90.6 0.0 copy-done
  90.6 0.0 copy-done.3
  90.6 0.0 copy-start.1
  90.6 1.0 %convolution_convert_fusion.1 = bf16[1024,128]{1,0:T(8,128)(2,1)} fusion(bf16[256,1024]{1,0:T(8,128)(2,1)S(1)} %copy-done, bf16[1,128,128]{2,1,0:T(8,128)(2,1)S(1)} %copy-done.3), kind=kOutput, calls=%fused_computation.1 | convolution fusion | flops 33685504 | bytes 557056 | tf_op jit(solution)/shard_map/jt,jk->tk/dot_general | solution.py:297
  91.6 0.0 copy-done.1
  91.6 0.7 slice_bitcast_fusion
Async XLA Ops:
  0.6 88.0 %copy-start.2 = (bf16[1,128,128]{2,1,0:T(8,128)(2,1)S(1)}, bf16[1,128,128]{2,1,0:T(8,128)(2,1)}, u32[]{:S(2)}) copy-start(bf16[1,128,128]{2,1,0:T(8,128)(2,1)} %fu.1) | copy-start | bytes 98308
  87.1 3.5 %copy-start = (bf16[256,1024]{1,0:T(8,128)(2,1)S(1)}, bf16[256,1024]{1,0:T(8,128)(2,1)}, u32[]{:S(2)}) copy-start(bf16[256,1024]{1,0:T(8,128)(2,1)} %get-tuple-element.9) | copy-start | bytes 1572868
  88.7 1.9 %copy-start.3 = (bf16[1,128,128]{2,1,0:T(8,128)(2,1)S(1)}, bf16[1,128,128]{2,1,0:T(8,128)(2,1)}, u32[]{:S(2)}) copy-start(bf16[1,128,128]{2,1,0:T(8,128)(2,1)} %sd.1) | copy-start | bytes 98308
  90.6 1.0 %copy-start.1 = (f32[4,64,256]{2,1,0:T(8,128)S(1)}, f32[4,64,256]{2,1,0:T(8,128)}, u32[]{:S(2)}) copy-start(f32[4,64,256]{2,1,0:T(8,128)} %get-tuple-element.11) | copy-start | bytes 786436
